TPU v7x, 32 devices: a whole 2x2x4 slice. The times are simulated.
32 devices in a mesh: space: 4 (over y, core), mode: 8 (over z, x).
Axes of the slice: x: 2, y: 2, z: 4, core: 2. Of those that a mesh axis runs over, the one named last changes fastest.
Arguments:
- intensity: float32 [1024, 8, 64, 256], P('mode', None, 'space'), may hold values from 0.1 to 2
- dir_cos: float32 [3, 32], replicated, may hold values from -1 to 1, as said below
- velocity: float32 [32], replicated, may hold values from 0.2 to 1
- rate: float32 [32], replicated, may hold values from 0.05 to 2
- spectrum: float32 [32], replicated, may hold values from 0.2 to 2
- weight: float32 [32], replicated, may hold values from 0.25 to 1.75
- heat: float32 [64, 256], P('space'), may hold values from 0.5 to 4
- rough_cells: int32 [4096], P('space'), may hold values from 0 to 4095, as said below
- rough_count: int32 [4], P('space'), may hold values from 256 to 1024, as said below
- rough_map: int32 [4096, 16], P('space'), may hold values from 0 to 15
Outputs:
- intensity_new: float32 [1024, 8, 64, 256], P('mode', None, 'space')
- energy_new: float32 [8, 64, 256], P(None, 'space')
Inputs may be any that keep to these rules, and one draw needn't show every extreme that they name: `dir_cos`: even directions have a positive third cosine, and direction 2k+1 equals direction 2k with the third cosine negated; every direction has a third cosine of magnitude 0.3 or more. `rough_cells`: the entries of one index of space are distinct. `rough_count`: some index of space has all 1024 slots live.
All inputs are finite; a program needn't handle non-finite values.
Results may differ from a plain program's by a relative error of at most 0.0015.
Values sent between devices are 32-bit elements; how exact they have to be, the bound alone decides.
A program may use at most 128 MiB of HBM per device.

v0:
```python
import functools

import jax
import jax.numpy as jnp
from jax import lax
from jax.experimental import pallas as pl
from jax.experimental.pallas import tpu as pltpu
from jax.sharding import PartitionSpec as P

MESH = pl.DeviceIdType.MESH
F32 = jnp.float32
BF16 = jnp.bfloat16


def whole(space=pltpu.VMEM):
    return pl.BlockSpec(memory_space=space)


def squash(energy):
    return energy / (1.0 + 0.3 * jnp.abs(energy))


def send(src, dst, ssem, rsem, axis, target):
    return pltpu.make_async_remote_copy(
        src_ref=src,
        dst_ref=dst,
        send_sem=ssem,
        recv_sem=rsem,
        device_id={axis: target},
        device_id_type=MESH,
    )


def reduce_all(acc, slots, part, total, sems, n, finish):
    me = lax.axis_index("mode")
    rows = acc.shape[0] // n

    def chunk(i):
        return pl.ds(pl.multiple_of(i * rows, rows), rows)

    first = []
    for off in range(1, n):
        target = lax.rem(me + off, n)
        copy = send(
            acc.at[chunk(target)], slots.at[off], sems.at[0, off], sems.at[1, off], "mode", target
        )
        copy.start()
        first.append(copy)
    for copy in first:
        copy.wait_recv()
    value = acc[chunk(me), :]
    for off in range(1, n):
        value = value + slots[off]
    part[...] = finish(value)
    second = []
    for off in range(1, n):
        target = lax.rem(me + off, n)
        copy = send(part, total.at[chunk(me)], sems.at[2, off], sems.at[3, off], "mode", target)
        copy.start()
        second.append(copy)
    total[chunk(me), :] = part[...]
    for copy in first:
        copy.wait_send()
    for off in range(1, n):
        source = lax.rem(me + n - off, n)
        send(
            part, total.at[chunk(source)], sems.at[2, off], sems.at[3, off], "mode", source
        ).wait_recv()
    for copy in second:
        copy.wait_send()


def greet_modes(barrier, n):
    me = lax.axis_index("mode")
    for off in range(1, n):
        pl.semaphore_signal(
            barrier, inc=1, device_id={"mode": lax.rem(me + off, n)}, device_id_type=MESH
        )


def open_kernel(
    n, ns, modes, planes, pairs_total,
    weight, x_ref, equil, lo_out, hi_out,
    acc, slots, part, total, row_first, row_last, hsem, sems,
):
    step = pl.program_id(0)
    steps = pl.num_programs(0)
    block = x_ref.shape[0]
    rows = x_ref.shape[1]
    per_plane = rows // planes
    me = lax.axis_index("mode")
    sp = lax.axis_index("space")
    dirs_local = lo_out.shape[0] // modes

    @pl.when(step == 0)
    def _():
        barrier = pltpu.get_barrier_semaphore()
        greet_modes(barrier, n)

        @pl.when(sp > 0)
        def _():
            pl.semaphore_signal(barrier, inc=1, device_id={"space": sp - 1}, device_id_type=MESH)

        @pl.when(sp < ns - 1)
        def _():
            pl.semaphore_signal(barrier, inc=1, device_id={"space": sp + 1}, device_id_type=MESH)

        low = jnp.where(sp > 0, 1, 0)
        high = jnp.where(sp < ns - 1, 1, 0)
        pl.semaphore_wait(barrier, n - 1 + low + high)
        acc[...] = jnp.zeros_like(acc)

    part_of = pl.ds(step * block, block)
    has_low = jnp.where(sp > 0, 1.0, 0.0)
    has_high = jnp.where(sp < ns - 1, 1.0, 0.0)

    def edges(p, carry):
        for z in range(planes):
            first, last = z * per_plane, (z + 1) * per_plane - 1
            row_first[step * block + p, pl.ds(z, 1), :] = x_ref[p, pl.ds(first, 1), :] * has_low
            row_last[step * block + p, pl.ds(z, 1), :] = x_ref[p, pl.ds(last, 1), :] * has_high
        return carry

    lax.fori_loop(0, block, edges, 0)

    def down_copy(g):
        where = pl.ds(g * block, block)
        return send(
            row_first.at[where], hi_out.at[where], hsem.at[0, g], hsem.at[1, g], "space",
            lax.rem(sp + ns - 1, ns),
        )

    def up_copy(g):
        where = pl.ds(g * block, block)
        return send(
            row_last.at[where], lo_out.at[where], hsem.at[2, g], hsem.at[3, g], "space",
            lax.rem(sp + 1, ns),
        )

    def low_zero(g):
        where = pl.ds(g * block, block)
        return pltpu.make_async_copy(row_first.at[where], lo_out.at[where], hsem.at[3, g])

    def high_zero(g):
        where = pl.ds(g * block, block)
        return pltpu.make_async_copy(row_last.at[where], hi_out.at[where], hsem.at[1, g])

    @pl.when(sp > 0)
    def _():
        down_copy(step).start()

    @pl.when(sp == 0)
    def _():
        low_zero(step).start()

    @pl.when(sp < ns - 1)
    def _():
        up_copy(step).start()

    @pl.when(sp == ns - 1)
    def _():
        high_zero(step).start()

    w = weight[me * dirs_local + step * block // modes]

    def add_rows(r, carry):
        here = pl.ds(pl.multiple_of(r * 8, 8), 8)
        value = x_ref[0, here, :]
        for p in range(1, block):
            value = value + x_ref[p, here, :]
        acc[here, :] += w * value
        return carry

    lax.fori_loop(0, rows // 8, add_rows, 0)

    @pl.when(step == steps - 1)
    def _():
        reduce_all(
            acc, slots, part, total, sems, n, lambda value: squash(value * (1.0 / pairs_total))
        )
        equil[...] = total[...]

        def finish(g, carry):
            @pl.when(sp > 0)
            def _():
                down_copy(g).wait_send()
                up_copy(g).wait_recv()

            @pl.when(sp == 0)
            def _():
                low_zero(g).wait()

            @pl.when(sp < ns - 1)
            def _():
                up_copy(g).wait_send()
                down_copy(g).wait_recv()

            @pl.when(sp == ns - 1)
            def _():
                high_zero(g).wait()

            return carry

        lax.fori_loop(0, lo_out.shape[0] // block, finish, 0)


def open_step(x, weight, n, ns, modes, planes, pairs_total):
    pairs, rows, width = x.shape
    block = 16
    halo = jax.ShapeDtypeStruct((pairs, planes, width), F32)
    return pl.pallas_call(
        functools.partial(open_kernel, n, ns, modes, planes, pairs_total),
        grid=(pairs // block,),
        out_shape=(jax.ShapeDtypeStruct((rows, width), F32), halo, halo),
        in_specs=[whole(pltpu.SMEM), pl.BlockSpec((block, rows, width), lambda i: (i, 0, 0))],
        out_specs=(pl.BlockSpec((rows, width), lambda i: (0, 0)), whole(pl.ANY), whole(pl.ANY)),
        scratch_shapes=[
            pltpu.VMEM((rows, width), F32),
            pltpu.VMEM((n, rows // n, width), F32),
            pltpu.VMEM((rows // n, width), F32),
            pltpu.VMEM((rows, width), F32),
            pltpu.VMEM((pairs, planes, width), F32),
            pltpu.VMEM((pairs, planes, width), F32),
            pltpu.SemaphoreType.DMA((4, pairs // block)),
            pltpu.SemaphoreType.DMA((4, n)),
        ],
        compiler_params=pltpu.CompilerParams(collective_id=0, has_side_effects=True),
        name="open_step",
    )(weight, x)


def close_kernel(n, pairs_total, x_ref, out, slots, part, total, sems):
    barrier = pltpu.get_barrier_semaphore()
    greet_modes(barrier, n)
    pl.semaphore_wait(barrier, n - 1)
    reduce_all(x_ref, slots, part, total, sems, n, lambda value: value * (1.0 / pairs_total))
    out[...] = total[...]


def close_step(x, n, pairs_total):
    rows, width = x.shape
    return pl.pallas_call(
        functools.partial(close_kernel, n, pairs_total),
        out_shape=jax.ShapeDtypeStruct((rows, width), F32),
        in_specs=[whole()],
        out_specs=whole(),
        scratch_shapes=[
            pltpu.VMEM((n, rows // n, width), F32),
            pltpu.VMEM((rows // n, width), F32),
            pltpu.VMEM((rows, width), F32),
            pltpu.SemaphoreType.DMA((4, n)),
        ],
        compiler_params=pltpu.CompilerParams(collective_id=1, has_side_effects=True),
        name="close_step",
    )(x)


def split(value):
    high = value.astype(BF16)
    return high, (value - high.astype(F32)).astype(BF16)


def rough_kernel(
    n, planes, count, dir_cos, velocity, rate, spectrum, bottom, cells, targets, equil, x, lo, hi,
    inflow, base, held, picked, marks, xin, loin, hiin, xout, ssem, rsem, lsem,
):
    me = lax.axis_index("mode")
    pairs, rows, width = bottom.shape
    slots = cells.shape[1]
    half = targets.shape[0]
    modes = pairs // half

    def place_of(index):
        return jnp.where(lax.rem(index, 2) == 0, index // 2, n - 1 - index // 2)

    def index_of(place):
        place = lax.rem(place + n, n)
        return jnp.where(place < n // 2, 2 * place, 2 * (n - 1 - place) + 1)

    place = place_of(me)
    ends = (index_of(place + 1), index_of(place - 1))
    barrier = pltpu.get_barrier_semaphore()
    for target in ends:
        pl.semaphore_signal(barrier, inc=1, device_id={"mode": target}, device_id_type=MESH)

    marks[...] = jnp.where(
        lax.broadcasted_iota(jnp.int32, (width, slots), 0) == lax.rem(cells[...], width), 1.0, 0.0
    ).astype(BF16)
    row_of = cells[...] // width
    on_row = jnp.where(lax.broadcasted_iota(jnp.int32, (rows, slots), 0) == row_of, 1.0, 0.0)

    piece = pairs // 4

    def rows_of(way, part):
        return (2 * way + part) * piece

    def gather(first):
        here = pl.ds(first, piece)
        high, low = split(bottom[here].reshape(piece * rows, width))
        column = marks[...]
        got = jnp.dot(high, column, preferred_element_type=F32) + jnp.dot(
            low, column, preferred_element_type=F32
        )
        held[place, here, :] = jnp.sum(got.reshape(piece, rows, slots) * on_row[None], axis=1)

    def slot_of(way, step):
        return lax.rem(place + n + (-step if way == 0 else step), n)

    def copy_of(way, part, step):
        at = held.at[slot_of(way, step), pl.ds(rows_of(way, part), piece)]
        return send(at, at, ssem.at[way, part, step], rsem.at[way, part, step], "mode", ends[way])

    def arrival(way, part, step):
        at = held.at[slot_of(way, step + 1), pl.ds(rows_of(way, part), piece)]
        return send(at, at, ssem.at[way, part, step], rsem.at[way, part, step], "mode", ends[way])

    def choose(way, step):
        slot = slot_of(way, step)
        owner = index_of(slot)
        for h in range(half):
            want = targets[pl.ds(h, 1), :]
            for first in range(rows_of(way, 0), rows_of(way, 0) + 2 * piece, 8):
                j, m = first // modes, first % modes
                here = pl.ds(h * modes + m, 8)
                picked[here, :] = jnp.where(
                    want == owner * half + j, held[slot, pl.ds(first, 8), :], picked[here, :]
                )

    batch = xin.shape[1]
    per_dir = modes // batch
    chunks = half * per_dir
    wide = min(4, batch)
    row = lax.broadcasted_iota(jnp.int32, (rows, width), 0)
    lane = lax.broadcasted_iota(jnp.int32, (rows, width), 1)

    def loads(c):
        at = (c // per_dir, 0, pl.ds((c % per_dir) * batch, batch))
        return [
            pltpu.make_async_copy(src.at[at], dst.at[c % 2], lsem.at[k, c % 2])
            for k, (src, dst) in enumerate(((x, xin), (lo, loin), (hi, hiin)))
        ]

    def store(c):
        at = (c // per_dir, pl.ds((c % per_dir) * batch, batch))
        return pltpu.make_async_copy(xout.at[c % 2], base.at[at], lsem.at[3, c % 2])

    def advance(c):
        for copy in loads(c):
            copy.wait()
        if c + 1 < chunks:
            for copy in loads(c + 1):
                copy.start()
        if c >= 2:
            store(c - 2).wait()
        slot = c % 2
        s = (me * half + c // per_dir) * 2
        cx, cy, cz = dir_cos[0, s], dir_cos[1, s], dir_cos[2, s]
        low_x = jnp.full((rows, width), cx, F32) >= 0.0
        low_y = jnp.full((rows, width), cy, F32) >= 0.0
        at_edge = (low_x & (row == 0)) | (~low_x & (row == rows - 1))
        at_side = (low_y & (lane == 0)) | (~low_y & (lane == width - 1))

        def some(g, carry):
            picks = [g * wide + t for t in range(wide)]
            own_k, x_k, y_k, src_k, prev_k, values = [], [], [], [], [], [None] * wide
            for i in picks:
                m = (c % per_dir) * batch + i
                v = velocity[m]
                turn = v * jnp.abs(cz)
                inv = 1.0 / jnp.full((rows, width), 1.0 + rate[m] + turn, F32)
                vx, vy = v * jnp.abs(cx), v * jnp.abs(cy)
                own_k.append(inv * (1.0 - vx - vy))
                x_k.append(inv * vx)
                y_k.append(inv * vy)
                src_k.append(inv * (rate[m] * spectrum[m]))
                prev_k.append(inv * turn)
            for z in range(planes):
                here = pl.ds(z * rows, rows)
                level = equil[here, :]
                for t, i in enumerate(picks):
                    own = xin[slot, i, here, :]
                    edge = jnp.where(
                        low_x,
                        jnp.broadcast_to(loin[slot, i, pl.ds(z, 1), :], (rows, width)),
                        jnp.broadcast_to(hiin[slot, i, pl.ds(z, 1), :], (rows, width)),
                    )
                    side = jnp.where(low_x, pltpu.roll(own, 1, 0), pltpu.roll(own, rows - 1, 0))
                    side = jnp.where(at_edge, edge, side)
                    along = jnp.where(low_y, pltpu.roll(own, 1, 1), pltpu.roll(own, width - 1, 1))
                    along = jnp.where(at_side, 0.0, along)
                    value = (
                        own_k[t] * own + x_k[t] * side + y_k[t] * along + src_k[t] * level
                    )
                    if values[t] is not None:
                        value = value + prev_k[t] * values[t]
                    values[t] = value
                    xout[slot, i, here, :] = value
            return carry

        lax.fori_loop(0, batch // wide, some, 0)
        store(c).start()

    for copy in loads(0):
        copy.start()
    for part in range(2):
        for way in range(2):
            gather(rows_of(way, part))
            if part == 0 and way == 0:
                pl.semaphore_wait(barrier, 2)
            copy_of(way, part, 0).start()
    picked[...] = jnp.zeros_like(picked)
    for way in range(2):
        choose(way, 0)
    for c in range(0, chunks // n):
        advance(c)
    for step in range(1, n):
        for part in range(2):
            for way in range(2):
                arrival(way, part, step - 1).wait_recv()
                if step < n - 1:
                    copy_of(way, part, step).start()
        for way in range(2):
            choose(way, step)
        for c in range(step * chunks // n, (step + 1) * chunks // n):
            advance(c)
    for step in range(n - 1):
        for part in range(2):
            for way in range(2):
                copy_of(way, part, step).wait_send()

    for c in range(max(0, chunks - 2), chunks):
        store(c).wait()
    group = piece
    live = jnp.where(lax.broadcasted_iota(jnp.int32, (rows, slots), 1) < count[0], on_row, 0.0)
    contract = (((1,), (1,)), ((), ()))
    is_rough = lax.dot_general(live.astype(BF16), marks[...], contract, preferred_element_type=F32)
    is_rough = (is_rough > 0.5)[None]

    def scatter(g, carry):
        here = pl.ds(pl.multiple_of(g * group, group), group)
        spread = (picked[here, :][:, None, :] * live[None]).reshape(group * rows, slots)
        high, low = split(spread)
        column = marks[...]
        put = lax.dot_general(
            high, column, contract, preferred_element_type=F32
        ) + lax.dot_general(low, column, contract, preferred_element_type=F32)
        inflow[here] = 0.9 * jnp.where(is_rough, put.reshape(group, rows, width), bottom[here])
        return carry

    lax.fori_loop(0, pairs // group, scatter, 0)


def rough_step(bottom, cells, count, targets, scalars, equil, x, lo, hi, n):
    pairs, rows, width = bottom.shape
    slots = cells.shape[1]
    half, _, modes, total_rows, _ = x.shape
    planes = total_rows // rows
    batch = min(8, modes)
    return pl.pallas_call(
        functools.partial(rough_kernel, n, planes),
        out_shape=(
            jax.ShapeDtypeStruct(bottom.shape, F32),
            jax.ShapeDtypeStruct((half, modes, total_rows, width), F32),
        ),
        in_specs=[whole(pltpu.SMEM)] * 5 + [whole()] * 4 + [whole(pl.ANY)] * 3,
        out_specs=(whole(), whole(pl.ANY)),
        scratch_shapes=[
            pltpu.VMEM((n, pairs, slots), F32),
            pltpu.VMEM((pairs, slots), F32),
            pltpu.VMEM((width, slots), BF16),
            pltpu.VMEM((2, batch, total_rows, width), F32),
            pltpu.VMEM((2, batch, planes, width), F32),
            pltpu.VMEM((2, batch, planes, width), F32),
            pltpu.VMEM((2, batch, total_rows, width), F32),
            pltpu.SemaphoreType.DMA((2, 2, n - 1)),
            pltpu.SemaphoreType.DMA((2, 2, n - 1)),
            pltpu.SemaphoreType.DMA((4, 2)),
        ],
        compiler_params=pltpu.CompilerParams(collective_id=2, has_side_effects=True),
        name="rough_step",
    )(count, *scalars[:4], bottom, cells, targets, equil, x, lo, hi)


def rise_kernel(planes, dir_cos, velocity, rate, weight, base, inflow, before, _, out, energy):
    h, b = pl.program_id(0), pl.program_id(1)
    count, total_rows, width = base.shape
    rows = total_rows // planes

    @pl.when((h == 0) & (b == 0))
    def _():
        energy[...] = before[...]

    s = (lax.axis_index("mode") * pl.num_programs(0) + h) * 2
    cz, w = dir_cos[2, s], weight[s]
    wide = min(4, count)

    def some(g, carry):
        picks = [g * wide + t for t in range(wide)]
        prev_k, values = [], []
        for i in picks:
            m = b * count + i
            turn = velocity[m] * jnp.abs(cz)
            ratio = jnp.full((rows, width), turn, F32) / jnp.full(
                (rows, width), 1.0 + rate[m] + turn, F32
            )
            prev_k.append(ratio)
            values.append(inflow[i])
        for z in range(planes):
            here = pl.ds(z * rows, rows)
            total = None
            for t, i in enumerate(picks):
                values[t] = prev_k[t] * values[t]
                value = base[i, here, :] + values[t]
                out[i, here, :] = value
                total = value if total is None else total + value
            energy[here, :] += w * total
        return carry

    lax.fori_loop(0, count // wide, some, 0)


def rise_step(planes, scalars, base, inflow, before, fresh):
    half, modes, total_rows, width = base.shape
    rows = total_rows // planes
    block = min(8, modes)
    dir_cos, velocity, rate, _, weight = scalars
    flat = pl.BlockSpec((total_rows, width), lambda h, b: (0, 0))
    return pl.pallas_call(
        functools.partial(rise_kernel, planes),
        grid=(half, modes // block),
        out_shape=(
            jax.ShapeDtypeStruct(fresh.shape, F32),
            jax.ShapeDtypeStruct((total_rows, width), F32),
        ),
        in_specs=[whole(pltpu.SMEM)] * 4
        + [
            pl.BlockSpec((None, block, total_rows, width), lambda h, b: (h, b, 0, 0)),
            pl.BlockSpec((None, block, rows, width), lambda h, b: (h, b, 0, 0)),
            flat,
            whole(pl.ANY),
        ],
        out_specs=(
            pl.BlockSpec((None, None, block, total_rows, width), lambda h, b: (h, 0, b, 0, 0)),
            flat,
        ),
        input_output_aliases={7: 0},
        name="rise_step",
    )(dir_cos, velocity, rate, weight, base, inflow, before, fresh)


def sweep_kernel(down, planes, *refs):
    if down:
        (dir_cos, velocity, rate, spectrum, weight, x_ref, lo, hi, equil, start, out, bottom,
         energy) = refs
    else:
        (dir_cos, velocity, rate, spectrum, weight, x_ref, lo, hi, equil, start, before, _,
         out, energy) = refs
    h, b = pl.program_id(0), pl.program_id(1)
    count, total_rows, width = x_ref.shape
    rows = total_rows // planes

    @pl.when((h == 0) & (b == 0))
    def _():
        energy[...] = jnp.zeros_like(energy) if down else before[...]

    s = (lax.axis_index("mode") * pl.num_programs(0) + h) * 2 + (1 if down else 0)
    cx, cy, cz = dir_cos[0, s], dir_cos[1, s], dir_cos[2, s]
    w = weight[s]
    row = lax.broadcasted_iota(jnp.int32, (rows, width), 0)
    lane = lax.broadcasted_iota(jnp.int32, (rows, width), 1)

    wide = min(4, count)

    def run(low_x, low_y):
        def some(g, carry):
            picks = [g * wide + t for t in range(wide)]
            own_k, x_k, y_k, src_k, prev_k, values = [], [], [], [], [], []
            for i in picks:
                m = b * count + i
                v = velocity[m]
                c = v * jnp.abs(cz)
                inv = 1.0 / jnp.full((rows, width), 1.0 + rate[m] + c, F32)
                vx, vy = v * jnp.abs(cx), v * jnp.abs(cy)
                own_k.append(inv * (1.0 - vx - vy))
                x_k.append(inv * vx)
                y_k.append(inv * vy)
                src_k.append(inv * (rate[m] * spectrum[m]))
                prev_k.append(inv * c)
                values.append(start[...] * spectrum[m] if down else start[i])
            for z in reversed(range(planes)) if down else range(planes):
                here = pl.ds(z * rows, rows)
                level = equil[here, :]
                total = None
                for t, i in enumerate(picks):
                    own = x_ref[i, here, :]
                    edge = (lo if low_x else hi)[i, pl.ds(z, 1), :]
                    if low_x:
                        side = jnp.where(row == 0, edge, pltpu.roll(own, 1, 0))
                    else:
                        side = jnp.where(row == rows - 1, edge, pltpu.roll(own, rows - 1, 0))
                    along = pltpu.roll(own, 1 if low_y else width - 1, 1)
                    along = jnp.where(lane == (0 if low_y else width - 1), 0.0, along)
                    value = (
                        own_k[t] * own + x_k[t] * side + y_k[t] * along + src_k[t] * level
                        + prev_k[t] * values[t]
                    )
                    values[t] = value
                    out[i, here, :] = value
                    total = value if total is None else total + value
                energy[here, :] += w * total
            if down:
                for t, i in enumerate(picks):
                    bottom[i] = values[t]
            return carry

        lax.fori_loop(0, count // wide, some, 0)

    for low_x in (True, False):
        for low_y in (True, False):
            @pl.when(((cx >= 0) == low_x) & ((cy >= 0) == low_y))
            def _():
                run(low_x, low_y)


def sweep_step(down, planes, scalars, x, lo, hi, equil, start, before=None, aliased=None):
    half, _, modes, total_rows, width = x.shape
    rows = total_rows // planes
    block = min(8, modes)
    side = 1 if down else 0
    big = pl.BlockSpec((None, None, block, total_rows, width), lambda h, b: (h, side, b, 0, 0))
    edge = pl.BlockSpec((None, None, block, planes, width), lambda h, b: (h, side, b, 0, 0))
    flat = pl.BlockSpec((total_rows, width), lambda h, b: (0, 0))
    floor = pl.BlockSpec((None, block, rows, width), lambda h, b: (h, b, 0, 0))
    heat = pl.BlockSpec((rows, width), lambda h, b: (0, 0))
    in_specs = [whole(pltpu.SMEM)] * len(scalars) + [big, edge, edge, flat]
    flat_shape = jax.ShapeDtypeStruct((total_rows, width), F32)
    floor_shape = jax.ShapeDtypeStruct((half, modes, rows, width), F32)
    args = [*scalars, x, lo, hi, equil, start]
    if down:
        in_specs += [heat]
        out_shape = (jax.ShapeDtypeStruct(x.shape, F32), floor_shape, flat_shape)
        out_specs = (big, floor, flat)
        aliases = {}
    else:
        in_specs += [floor, flat, whole(pl.ANY)]
        args += [before, aliased]
        out_shape = (jax.ShapeDtypeStruct(x.shape, F32), flat_shape)
        out_specs = (big, flat)
        aliases = {len(args) - 1: 0}
    return pl.pallas_call(
        functools.partial(sweep_kernel, down, planes),
        grid=(half, modes // block),
        out_shape=out_shape,
        in_specs=in_specs,
        out_specs=out_specs,
        input_output_aliases=aliases,
        name="down_sweep" if down else "up_sweep",
    )(*args)


def per_device(
    n, ns, intensity, dir_cos, velocity, rate, spectrum, weight, heat, rough_cells, rough_count,
    rough_map,
):
    pairs, planes, rows, width = intensity.shape
    modes = velocity.shape[0]
    half = pairs // modes // 2
    pairs_total = pairs * n
    position = lax.axis_index("mode")
    flat = intensity.reshape(pairs, planes * rows, width)
    equil, lo, hi = open_step(flat, weight, n, ns, modes, planes, pairs_total)
    x = intensity.reshape(half, 2, modes, planes * rows, width)
    lo = lo.reshape(half, 2, modes, planes, width)
    hi = hi.reshape(half, 2, modes, planes, width)
    scalars = (dir_cos, velocity, rate, spectrum, weight)
    fresh, bottom, energy = sweep_step(True, planes, scalars, x, lo, hi, equil, heat)
    targets = lax.dynamic_slice_in_dim(rough_map, position * half, half, 1).T
    inflow, base = rough_step(
        bottom.reshape(half * modes, rows, width), rough_cells[None], rough_count, targets,
        scalars, equil, x, lo, hi, n,
    )
    inflow = inflow.reshape(half, modes, rows, width)
    fresh, energy = rise_step(planes, scalars, base, inflow, energy, fresh)
    energy = close_step(energy, n, pairs_total)
    return fresh.reshape(intensity.shape), energy.reshape(planes, rows, width)


def solution(mesh):
    n, ns = mesh.shape["mode"], mesh.shape["space"]
    in_specs = (
        P("mode", None, "space", None),
        P(),
        P(),
        P(),
        P(),
        P(),
        P("space", None),
        P("space"),
        P("space"),
        P("space", None),
    )
    out_specs = (P("mode", None, "space", None), P(None, "space", None))
    return jax.shard_map(
        functools.partial(per_device, n, ns),
        mesh=mesh,
        in_specs=in_specs,
        out_specs=out_specs,
        check_vma=False,
    )
```

profile of v0, /device:TPU:0, one launch (start us, length us, event | category | flops | bytes accessed | tf_op | source)
XLA Modules:
  0.0 99.9 jit_solution(3139790689584296658)
XLA Ops:
  0.6 0.0 copy-start
  1.3 0.1 copy-done
  1.5 0.6 dynamic-slice_bitcast_fusion.targets
  2.1 26.6 %open_step.1 = (f32[128,256]{1,0:T(8,128)}, f32[128,8,256]{2,1,0:T(8,128)}, f32[128,8,256]{2,1,0:T(8,128)}) custom-call(f32[32]{0:T(128)} %weight.3, f32[128,128,256]{2,1,0:T(8,128)} %bitcast.11), custom_call_target="tpu_custom_call" | custom-call | tf_op jit(solution)/shard_map/open_step/pallas_call | solution.py:211
  28.7 11.7 %down_sweep.1 = (f32[2,2,32,128,256]{4,3,2,1,0:T(8,128)}, f32[2,32,16,256]{3,2,1,0:T(8,128)}, f32[128,256]{1,0:T(8,128)}) custom-call(f32[3,32]{1,0:T(4,128)} %dir_cos.3, f32[32]{0:T(128)} %velocity.3, f32[32]{0:T(128)} %rate.3, f32[32]{0:T(128)} %spectrum.1, f32[32]{0:T(128)} %weight.3, f32[2,2,32,128,256]{4,3,2,1,0:T(8,128)} %bitcast.12, ...), custom_call_target="tpu_custom_call" | custom-call | tf_op jit(solution)/shard_map/down_sweep/pallas_call | solution.py:650
  40.4 35.2 %rough_step.1 = (f32[64,16,256]{2,1,0:T(8,128)}, f32[2,32,128,256]{3,2,1,0:T(8,128)}) custom-call(s32[1]{0:T(128)S(6)} %copy.15.count, f32[3,32]{1,0:T(4,128)} %dir_cos.3, f32[32]{0:T(128)} %velocity.3, f32[32]{0:T(128)} %rate.3, f32[32]{0:T(128)} %spectrum.1, f32[64,16,256]{2,1,0:T(8,128)} %bitcast.20, s32[1,1024]{1,0:T(1,128)} %bitcast.22, ...), custom_call_target="tpu_custom_call" | custom-call | tf_op jit(solution)/shard_map/rough_step/pallas_call | solution.py:459
  75.6 9.5 %rise_step.1 = (f32[2,2,32,128,256]{4,3,2,1,0:T(8,128)}, f32[128,256]{1,0:T(8,128)}) custom-call(f32[3,32]{1,0:T(4,128)} %dir_cos.3, f32[32]{0:T(128)} %velocity.3, f32[32]{0:T(128)} %rate.3, f32[32]{0:T(128)} %weight.3, f32[2,32,128,256]{3,2,1,0:T(8,128)} %get-tuple-element.16.base, f32[2,32,16,256]{3,2,1,0:T(8,128)} %bitcast.19, ...), custom_call_target="tpu_custom_call", output_to_operand_aliasing={{0}: (7, {})} | custom-call | tf_op jit(solution)/shard_map/rise_step/pallas_call | solution.py:528
  85.1 13.2 %close_step.1 = f32[128,256]{1,0:T(8,128)} custom-call(f32[128,256]{1,0:T(8,128)} %get-tuple-element.21.x_ref), custom_call_target="tpu_custom_call" | custom-call | tf_op jit(solution)/shard_map/close_step/pallas_call | solution.py:242
  98.3 1.6 %copy.16 = f32[8,16,256]{2,1,0:T(8,128)} copy(f32[8,16,256]{2,1,0:T(8,128)} %bitcast.21) | data formatting | bytes 262144
Async XLA Ops:
  0.6 0.8 copy-start
where the time goes:
time: 101 us; the launch traced here: 99.9 us
  Pallas kernels  96.2 us (95%)
  local copies, waits for them, and re-layouts  2.32 us (2%)
  between operations  1.35 us (1%)
    pallas_call x1, Pallas kernels, rough_step(): pl.pallas_call(functools.partial(rough_kernel, n, planes), out_shape=(jax...  35.2 us
    pallas_call x1, Pallas kernels, open_step(): pl.pallas_call(functools.partial(open_kernel, n, ns, modes, planes, pairs...  26.6 us
    pallas_call x1, Pallas kernels, close_step(): pl.pallas_call(functools.partial(close_kernel, n, pairs_total), out_shape...  13.2 us
    pallas_call x1, Pallas kernels, sweep_step(): pl.pallas_call(functools.partial(sweep_kernel, down, planes), grid=(half,...  11.7 us
    pallas_call x1, Pallas kernels, rise_step(): pl.pallas_call(functools.partial(rise_kernel, planes), grid=(half, modes...  9.54 us

commit v1 on v0

v1 whole, which is shorter than its diff:
```python
import functools

import jax
import jax.numpy as jnp
from jax import lax
from jax.experimental import pallas as pl
from jax.experimental.pallas import tpu as pltpu
from jax.sharding import PartitionSpec as P

MESH = pl.DeviceIdType.MESH
F32 = jnp.float32
BF16 = jnp.bfloat16
SUB, LANE = 8, 128
MIB = 1 << 20


def whole(space=pltpu.VMEM):
    return pl.BlockSpec(memory_space=space)


def squash(energy):
    return energy / (1.0 + 0.3 * jnp.abs(energy))


def send(src, dst, ssem, rsem, axis, target):
    return pltpu.make_async_remote_copy(
        src_ref=src,
        dst_ref=dst,
        send_sem=ssem,
        recv_sem=rsem,
        device_id={axis: target},
        device_id_type=MESH,
    )


class Reduction:
    def __init__(self, acc, slots, part, total, sems, n):
        self.acc, self.slots, self.part, self.total = acc, slots, part, total
        self.sems, self.n = sems, n
        self.me = lax.axis_index("mode")
        self.rows = acc.shape[0] // n

    def chunk(self, i):
        return pl.ds(pl.multiple_of(i * self.rows, self.rows), self.rows)

    def outward(self, off):
        target = lax.rem(self.me + off, self.n)
        return send(
            self.acc.at[self.chunk(target)], self.slots.at[off],
            self.sems.at[0, off], self.sems.at[1, off], "mode", target,
        )

    def spread(self, off):
        target = lax.rem(self.me + off, self.n)
        return send(
            self.part, self.total.at[self.chunk(self.me)],
            self.sems.at[2, off], self.sems.at[3, off], "mode", target,
        )

    def start(self):
        for off in range(1, self.n):
            self.outward(off).start()

    def combine(self, finish):
        for off in range(1, self.n):
            self.outward(off).wait_recv()
        value = self.acc[self.chunk(self.me), :]
        for off in range(1, self.n):
            value = value + self.slots[off]
        self.part[...] = finish(value)
        for off in range(1, self.n):
            self.spread(off).start()
        self.total[self.chunk(self.me), :] = self.part[...]

    def finish(self):
        for off in range(1, self.n):
            source = lax.rem(self.me + self.n - off, self.n)
            send(
                self.part, self.total.at[self.chunk(source)],
                self.sems.at[2, off], self.sems.at[3, off], "mode", source,
            ).wait_recv()
        for off in range(1, self.n):
            self.outward(off).wait_send()
            self.spread(off).wait_send()


def split(value):
    high = value.astype(BF16)
    return high, (value - high.astype(F32)).astype(BF16)


def splat(value):
    return jnp.full((SUB, LANE), value, F32)


def tiles(rows, width):
    return [(r, c) for r in range(0, rows, SUB) for c in range(0, width, LANE)]


def main_kernel(
    n, ns, planes,
    count, dir_cos, velocity, rate, spectrum, weight, heat, cells, reflect, x,
    xv, inflow, energy,
    lo, hi, first, last, acc, slots1, part1, equil, acc2, slots2, part2,
    held, picked, marks, lsem, hsem, sems1, sems2, ssem, rsem,
):
    me, sp = lax.axis_index("mode"), lax.axis_index("space")
    pairs, total_rows, width = xv.shape
    rows = total_rows // planes
    modes = velocity.shape[0]
    dirs = pairs // modes
    half = dirs // 2
    quiet = half * modes
    pairs_total = pairs * n
    rough = cells.shape[1]
    batch = min(16, modes)
    per_dir = modes // batch
    order = [d for d in range(1, dirs, 2)] + [d for d in range(0, dirs, 2)]
    chunks = [(d, b) for d in order for b in range(per_dir)]

    def load(i):
        d, b = chunks[i]
        where = pl.ds(d * modes + b * batch, batch)
        return pltpu.make_async_copy(x.at[where], xv.at[where], lsem.at[i])

    for i in range(len(chunks)):
        load(i).start()

    def place_of(index):
        return jnp.where(lax.rem(index, 2) == 0, index // 2, n - 1 - index // 2)

    def index_of(place):
        place = lax.rem(place + n, n)
        return jnp.where(place < n // 2, 2 * place, 2 * (n - 1 - place) + 1)

    place = place_of(me)
    ends = (index_of(place + 1), index_of(place - 1))

    barrier = pltpu.get_barrier_semaphore()
    for off in range(1, n):
        pl.semaphore_signal(
            barrier, inc=1, device_id={"mode": lax.rem(me + off, n)}, device_id_type=MESH
        )

    @pl.when(sp > 0)
    def _():
        pl.semaphore_signal(barrier, inc=1, device_id={"space": sp - 1}, device_id_type=MESH)

    @pl.when(sp < ns - 1)
    def _():
        pl.semaphore_signal(barrier, inc=1, device_id={"space": sp + 1}, device_id_type=MESH)

    @pl.when(sp == 0)
    def _():
        lo[...] = jnp.zeros_like(lo)

    @pl.when(sp == ns - 1)
    def _():
        hi[...] = jnp.zeros_like(hi)

    acc[...] = jnp.zeros_like(acc)
    acc2[...] = jnp.zeros_like(acc2)
    marks[...] = jnp.where(
        lax.broadcasted_iota(jnp.int32, (width, rough), 0) == lax.rem(cells[...], width), 1.0, 0.0
    ).astype(BF16)

    low = jnp.where(sp > 0, 1, 0)
    high = jnp.where(sp < ns - 1, 1, 0)
    pl.semaphore_wait(barrier, n - 1 + low + high)

    def down_copy(i):
        d, b = chunks[i]
        where = pl.ds(d * modes + b * batch, batch)
        return send(
            first.at[where], hi.at[where], hsem.at[0, i], hsem.at[1, i], "space",
            lax.rem(sp + ns - 1, ns),
        )

    def up_copy(i):
        d, b = chunks[i]
        where = pl.ds(d * modes + b * batch, batch)
        return send(
            last.at[where], lo.at[where], hsem.at[2, i], hsem.at[3, i], "space",
            lax.rem(sp + 1, ns),
        )

    for i, (d, b) in enumerate(chunks):
        base = d * modes + b * batch
        load(i).wait()

        def edges(t, carry):
            p = base + t
            for z in range(planes):
                first[p, pl.ds(z, 1), :] = xv[p, pl.ds(z * rows, 1), :]
                last[p, pl.ds(z, 1), :] = xv[p, pl.ds((z + 1) * rows - 1, 1), :]
            return carry

        lax.fori_loop(0, batch, edges, 0)

        @pl.when(sp > 0)
        def _():
            down_copy(i).start()

        @pl.when(sp < ns - 1)
        def _():
            up_copy(i).start()

        w = weight[me * dirs + d]

        def add_rows(r, carry):
            here = pl.ds(pl.multiple_of(r * SUB, SUB), SUB)
            value = xv[base, here, :]
            for t in range(1, batch):
                value = value + xv[base + t, here, :]
            acc[here, :] += w * value
            return carry

        lax.fori_loop(0, total_rows // SUB, add_rows, 0)

    opening = Reduction(acc, slots1, part1, equil, sems1, n)
    opening.start()

    row = lax.broadcasted_iota(jnp.int32, (SUB, LANE), 0)
    lane = lax.broadcasted_iota(jnp.int32, (SUB, LANE), 1)
    places = tiles(rows, width)
    last_row, last_col = rows - SUB, width - LANE

    def factors(d, m):
        s = me * dirs + d
        v = velocity[m]
        turn = v * jnp.abs(dir_cos[2, s])
        inv = 1.0 / splat(1.0 + rate[m] + turn)
        return v * jnp.abs(dir_cos[0, s]), v * jnp.abs(dir_cos[1, s]), turn, inv

    def sweep(d, start, stop):
        s = me * dirs + d
        low_x, low_y = splat(dir_cos[0, s]) >= 0.0, splat(dir_cos[1, s]) >= 0.0
        shift_x = jnp.where(dir_cos[0, s] >= 0.0, 1, SUB - 1)
        shift_y = jnp.where(dir_cos[1, s] >= 0.0, 1, LANE - 1)
        wrap_x = (low_x & (row == 0)) | (~low_x & (row == SUB - 1))
        wrap_y = (low_y & (lane == 0)) | (~low_y & (lane == LANE - 1))
        wide = 2

        def some(g, carry):
            sets = []
            for t in range(wide):
                m = start + g * wide + t
                vx, vy, turn, inv = factors(d, m)
                kx, ky = inv * vx, inv * vy
                sets.append((
                    d * modes + m, inv * (1.0 - vx - vy), kx, ky, inv * turn,
                    jnp.where(low_x & (row == 0), 0.0, kx),
                    jnp.where(~low_x & (row == SUB - 1), 0.0, kx),
                    jnp.where(low_y & (lane == 0), 0.0, ky),
                    jnp.where(~low_y & (lane == LANE - 1), 0.0, ky),
                ))
            before = [None] * wide
            for z in range(planes) if d % 2 == 0 else reversed(range(planes)):
                for t in range(wide):
                    p, k0, kx, ky, kp, kx_top, kx_end, ky_top, ky_end = sets[t]
                    own = {
                        (r, c): xv[p, pl.ds(z * rows + r, SUB), pl.ds(c, LANE)] for r, c in places
                    }
                    side = {at: pltpu.roll(own[at], shift_x, 0) for at in places}
                    along = {at: pltpu.roll(own[at], shift_y, 1) for at in places}
                    now = {}
                    for r, c in places:
                        one = side[r, c]
                        if rows > SUB:
                            below = side[(r - SUB) % rows, c]
                            above = side[(r + SUB) % rows, c]
                            one = jnp.where(wrap_x, jnp.where(low_x, below, above), one)
                        two = along[r, c]
                        if width > LANE:
                            left = along[r, (c - LANE) % width]
                            right = along[r, (c + LANE) % width]
                            two = jnp.where(wrap_y, jnp.where(low_y, left, right), two)
                        gain_x = kx
                        if r == 0:
                            gain_x = kx_top
                        if r == last_row:
                            gain_x = kx_end if r else jnp.where(wrap_x, 0.0, kx)
                        gain_y = ky
                        if c == 0:
                            gain_y = ky_top
                        if c == last_col:
                            gain_y = ky_end if c else jnp.where(wrap_y, 0.0, ky)
                        value = k0 * own[r, c] + gain_x * one + gain_y * two
                        if before[t] is not None:
                            value = value + kp * before[t][r, c]
                        now[r, c] = value
                        xv[p, pl.ds(z * rows + r, SUB), pl.ds(c, LANE)] = value
                    before[t] = now
            return carry

        lax.fori_loop(0, (stop - start) // wide, some, 0)

    def settle(d, start, stop):
        s = me * dirs + d
        low_x = splat(dir_cos[0, s]) >= 0.0
        w = weight[s]
        wide = min(4, stop - start)

        def some(g, carry):
            sets = []
            for t in range(wide):
                m = start + g * wide + t
                vx, _, turn, inv = factors(d, m)
                kx = inv * vx
                sets.append((
                    d * modes + m, inv * turn, inv * (rate[m] * spectrum[m]),
                    jnp.where(low_x & (row == 0), kx, 0.0),
                    jnp.where(~low_x & (row == SUB - 1), kx, 0.0),
                ))
            values = []
            for t in range(wide):
                m = start + g * wide + t
                values.append({
                    (r, c): heat[pl.ds(r, SUB), pl.ds(c, LANE)] * spectrum[m] if d % 2 else None
                    for r, c in places
                })
            for z in range(planes) if d % 2 == 0 else reversed(range(planes)):
                for r, c in places:
                    here, cols = pl.ds(z * rows + r, SUB), pl.ds(c, LANE)
                    level = equil[here, cols]
                    total = None
                    for t in range(wide):
                        p, kp, ks, k_low, k_high = sets[t]
                        value = ks * level
                        if values[t][r, c] is not None:
                            value = value + kp * values[t][r, c]
                        if r == 0:
                            edge = lo[p, pl.ds(z, 1), cols]
                            value = value + k_low * jnp.broadcast_to(edge, (SUB, LANE))
                        if r == last_row:
                            edge = hi[p, pl.ds(z, 1), cols]
                            value = value + k_high * jnp.broadcast_to(edge, (SUB, LANE))
                        values[t][r, c] = value
                        out = xv[p, here, cols] + value
                        xv[p, here, cols] = out
                        total = out if total is None else total + out
                    acc2[here, cols] += w * total
            return carry

        lax.fori_loop(0, (stop - start) // wide, some, 0)

    def halo_wait(i):
        @pl.when(sp > 0)
        def _():
            down_copy(i).wait_send()
            up_copy(i).wait_recv()

        @pl.when(sp < ns - 1)
        def _():
            up_copy(i).wait_send()
            down_copy(i).wait_recv()

    for d in range(1, dirs, 2):
        sweep(d, 0, modes)
    opening.combine(lambda value: squash(value * (1.0 / pairs_total)))
    for d in range(0, dirs, 2):
        sweep(d, 0, modes)
    opening.finish()

    row_of = cells[...] // width
    on_row = jnp.where(lax.broadcasted_iota(jnp.int32, (rows, rough), 0) == row_of, 1.0, 0.0)
    piece = quiet // 4

    def rows_of(way, part):
        return (2 * way + part) * piece

    def pair_of(q):
        return (2 * (q // modes) + 1) * modes + q % modes

    def gather(q):
        bottom = xv[pl.ds(pair_of(q), piece), pl.ds(0, rows), :]
        high, low = split(bottom.reshape(piece * rows, width))
        column = marks[...]
        got = jnp.dot(high, column, preferred_element_type=F32) + jnp.dot(
            low, column, preferred_element_type=F32
        )
        held[place, pl.ds(q, piece), :] = jnp.sum(
            got.reshape(piece, rows, rough) * on_row[None], axis=1
        )

    def slot_of(way, step):
        return lax.rem(place + n + (-step if way == 0 else step), n)

    def copy_of(way, part, step):
        at = held.at[slot_of(way, step), pl.ds(rows_of(way, part), piece)]
        return send(at, at, ssem.at[way, part, step], rsem.at[way, part, step], "mode", ends[way])

    def arrival(way, part, step):
        at = held.at[slot_of(way, step + 1), pl.ds(rows_of(way, part), piece)]
        return send(at, at, ssem.at[way, part, step], rsem.at[way, part, step], "mode", ends[way])

    def choose(way, step):
        slot = slot_of(way, step)
        owner = index_of(slot)
        for h in range(half):
            want = reflect[pl.ds(me * half + h, 1), :]
            for q in range(rows_of(way, 0), rows_of(way, 0) + 2 * piece, SUB):
                j, m = q // modes, q % modes
                here = pl.ds(h * modes + m, SUB)
                picked[here, :] = jnp.where(
                    want == owner * half + j, held[slot, pl.ds(q, SUB), :], picked[here, :]
                )

    picked[...] = jnp.zeros_like(picked)
    waited = set()
    for part in range(2):
        for way in range(2):
            q = rows_of(way, part)
            d, m = 2 * (q // modes) + 1, q % modes
            for i, (dd, b) in enumerate(chunks):
                if dd == d and b * batch < m + piece and m < (b + 1) * batch and i not in waited:
                    waited.add(i)
                    halo_wait(i)
            settle(d, m, m + piece)
            gather(q)
            copy_of(way, part, 0).start()
    for i in range(len(chunks)):
        if i not in waited:
            halo_wait(i)
    for way in range(2):
        choose(way, 0)

    tasks = [(d, m) for d in range(0, dirs, 2) for m in range(0, modes, SUB)]
    per_step = -(-len(tasks) // (n - 2))
    for step in range(1, n):
        for part in range(2):
            for way in range(2):
                arrival(way, part, step - 1).wait_recv()
                if step < n - 1:
                    copy_of(way, part, step).start()
        for way in range(2):
            choose(way, step)
        for d, m in tasks[(step - 1) * per_step : step * per_step]:
            settle(d, m, m + SUB)
    for step in range(n - 1):
        for part in range(2):
            for way in range(2):
                copy_of(way, part, step).wait_send()

    live = jnp.where(lax.broadcasted_iota(jnp.int32, (rows, rough), 1) < count[0], on_row, 0.0)
    contract = (((1,), (1,)), ((), ()))
    is_rough = lax.dot_general(live.astype(BF16), marks[...], contract, preferred_element_type=F32)
    is_rough = (is_rough > 0.5)[None]

    def scatter(g, carry):
        q = pl.multiple_of(g * piece, piece)
        spread = (picked[pl.ds(q, piece), :][:, None, :] * live[None]).reshape(piece * rows, rough)
        high, low = split(spread)
        column = marks[...]
        put = lax.dot_general(
            high, column, contract, preferred_element_type=F32
        ) + lax.dot_general(low, column, contract, preferred_element_type=F32)
        bottom = xv[pl.ds(pair_of(q), piece), pl.ds(0, rows), :]
        inflow[pl.ds(q, piece)] = 0.9 * jnp.where(
            is_rough, put.reshape(piece, rows, width), bottom
        )
        return carry

    lax.fori_loop(0, quiet // piece, scatter, 0)

    def rise(h):
        d = 2 * h
        w = weight[me * dirs + d]
        wide = 4

        def some(g, carry):
            sets, values = [], []
            for t in range(wide):
                m = g * wide + t
                _, _, turn, inv = factors(d, m)
                sets.append(inv * turn)
                values.append({
                    (r, c): inflow[h * modes + m, pl.ds(r, SUB), pl.ds(c, LANE)] for r, c in places
                })
            for z in range(planes):
                for r, c in places:
                    here, cols = pl.ds(z * rows + r, SUB), pl.ds(c, LANE)
                    total = None
                    for t in range(wide):
                        value = sets[t] * values[t][r, c]
                        values[t][r, c] = value
                        total = value if total is None else total + value
                    acc2[here, cols] += w * total
            return carry

        lax.fori_loop(0, modes // wide, some, 0)

    for h in range(half):
        rise(h)
    closing = Reduction(acc2, slots2, part2, energy, sems2, n)
    closing.start()
    closing.combine(lambda value: value * (1.0 / pairs_total))
    closing.finish()


def main_step(scalars, count, heat, cells, reflect, x, n, ns, planes):
    pairs, total_rows, width = x.shape
    rows = total_rows // planes
    modes = scalars[1].shape[0]
    quiet = pairs // 2
    rough = cells.shape[1]
    n_chunks = (pairs // modes) * (modes // min(16, modes))
    flat = (total_rows, width)
    part = (total_rows // n, width)
    halo = pltpu.VMEM((pairs, planes, width), F32)
    return pl.pallas_call(
        functools.partial(main_kernel, n, ns, planes),
        out_shape=(
            jax.ShapeDtypeStruct(x.shape, F32),
            jax.ShapeDtypeStruct((quiet, rows, width), F32),
            jax.ShapeDtypeStruct(flat, F32),
        ),
        in_specs=[whole(pltpu.SMEM)] * 6 + [whole()] * 3 + [whole(pltpu.HBM)],
        out_specs=(whole(),) * 3,
        scratch_shapes=[
            halo, halo, halo, halo,
            pltpu.VMEM(flat, F32),
            pltpu.VMEM((n, *part), F32),
            pltpu.VMEM(part, F32),
            pltpu.VMEM(flat, F32),
            pltpu.VMEM(flat, F32),
            pltpu.VMEM((n, *part), F32),
            pltpu.VMEM(part, F32),
            pltpu.VMEM((n, quiet, rough), F32),
            pltpu.VMEM((quiet, rough), F32),
            pltpu.VMEM((width, rough), BF16),
            pltpu.SemaphoreType.DMA((n_chunks,)),
            pltpu.SemaphoreType.DMA((4, n_chunks)),
            pltpu.SemaphoreType.DMA((4, n)),
            pltpu.SemaphoreType.DMA((4, n)),
            pltpu.SemaphoreType.DMA((2, 2, n - 1)),
            pltpu.SemaphoreType.DMA((2, 2, n - 1)),
        ],
        compiler_params=pltpu.CompilerParams(
            collective_id=0, has_side_effects=True, vmem_limit_bytes=30 * MIB
        ),
        name="main_step",
    )(count, *scalars, heat, cells, reflect, x)


def emit_kernel(
    planes, dir_cos, velocity, rate, xv, inflow, summed, out, energy, rising, sem
):
    pairs, total_rows, width = xv.shape
    rows = total_rows // planes
    modes = velocity.shape[0]
    dirs = pairs // modes
    batch = min(8, modes)
    me = lax.axis_index("mode")
    places = tiles(rows, width)

    def whole_dir(d):
        where = pl.ds(d * modes, modes)
        return pltpu.make_async_copy(xv.at[where], out.at[where], sem.at[d, 0])

    def piece(d, b):
        return pltpu.make_async_copy(
            rising.at[pl.ds(d // 2 * modes + b * batch, batch)],
            out.at[pl.ds(d * modes + b * batch, batch)], sem.at[d, b],
        )

    for d in range(1, dirs, 2):
        whole_dir(d).start()
    energy[...] = summed[...]
    for d in range(0, dirs, 2):
        cz = jnp.abs(dir_cos[2, me * dirs + d])
        for b in range(modes // batch):
            def one(i, carry):
                m = b * batch + i
                turn = velocity[m] * cz
                ratio = splat(turn) / splat(1.0 + rate[m] + turn)
                q = d // 2 * modes + m
                for r, c in places:
                    cols = pl.ds(c, LANE)
                    value = inflow[q, pl.ds(r, SUB), cols]
                    for z in range(planes):
                        here = pl.ds(z * rows + r, SUB)
                        value = ratio * value
                        rising[q, here, cols] = xv[d * modes + m, here, cols] + value
                return carry

            lax.fori_loop(0, batch, one, 0)
            piece(d, b).start()
    for d in range(dirs):
        if d % 2:
            whole_dir(d).wait()
        else:
            for b in range(modes // batch):
                piece(d, b).wait()


def emit_step(planes, scalars, xv, inflow, summed):
    pairs, total_rows, width = xv.shape
    modes = scalars[1].shape[0]
    return pl.pallas_call(
        functools.partial(emit_kernel, planes),
        out_shape=(
            jax.ShapeDtypeStruct(xv.shape, F32),
            jax.ShapeDtypeStruct(summed.shape, F32),
        ),
        in_specs=[whole(pltpu.SMEM)] * 3 + [whole()] * 3,
        out_specs=(whole(pltpu.HBM), whole()),
        scratch_shapes=[
            pltpu.VMEM((pairs // 2, total_rows, width), F32),
            pltpu.SemaphoreType.DMA((pairs // modes, modes // min(8, modes))),
        ],
        compiler_params=pltpu.CompilerParams(vmem_limit_bytes=16 * MIB),
        name="emit_step",
    )(*scalars[:3], xv, inflow, summed)


def per_device(
    n, ns, intensity, dir_cos, velocity, rate, spectrum, weight, heat, rough_cells, rough_count,
    rough_map,
):
    pairs, planes, rows, width = intensity.shape
    x = intensity.reshape(pairs, planes * rows, width)
    scalars = (dir_cos, velocity, rate, spectrum, weight)
    xv, inflow, summed = main_step(
        scalars, rough_count, heat, rough_cells[None], rough_map.T, x, n, ns, planes
    )
    fresh, energy = emit_step(planes, scalars, xv, inflow, summed)
    return fresh.reshape(intensity.shape), energy.reshape(planes, rows, width)


def solution(mesh):
    n, ns = mesh.shape["mode"], mesh.shape["space"]
    in_specs = (
        P("mode", None, "space", None),
        P(),
        P(),
        P(),
        P(),
        P(),
        P("space", None),
        P("space"),
        P("space"),
        P("space", None),
    )
    out_specs = (P("mode", None, "space", None), P(None, "space", None))
    return jax.shard_map(
        functools.partial(per_device, n, ns),
        mesh=mesh,
        in_specs=in_specs,
        out_specs=out_specs,
        check_vma=False,
    )
```

time: 101 us -> 77 us (0.76)
  Pallas kernels: 96.2 us -> 69.9 us
  local copies, waits for them, and re-layouts: 2.32 us -> 5.54 us
    pallas_call x5 -> x2, Pallas kernels: 96.2 us -> 69.9 us  [the longest x1 62.7 us: main_step(): pl.pallas_call(functools.partial(main_kernel, n, ns, planes), out_shape=(...]
    unnamed x3 -> x16, local copies, waits for them, and re-layouts: 1.73 us -> 5.54 us
where the time goes in v1:
time: 77 us; the launch traced here: 76.7 us
  Pallas kernels  69.9 us (91%)
  local copies, waits for them, and re-layouts  5.54 us (7%)
  between operations  1.3 us (2%)
    pallas_call x1, Pallas kernels, main_step(): pl.pallas_call(functools.partial(main_kernel, n, ns, planes), out_shape=(...  62.7 us
    pallas_call x1, Pallas kernels, emit_step(): pl.pallas_call(functools.partial(emit_kernel, planes), out_shape=(jax.Sha...  7.19 us
    unnamed x16, local copies, waits for them, and re-layouts  5.54 us

profile of v1, /device:TPU:0, one launch (start us, length us, event | category | flops | bytes accessed | tf_op | source)
XLA Modules:
  0.0 76.7 jit_solution(16795176933396173988)
XLA Ops:
  1.3 0.0 copy-start
  1.3 0.8 %copy-done = s32[1024,16]{0,1:T(8,128)S(1)} copy-done((s32[1024,16]{0,1:T(8,128)S(1)}, s32[1024,16]{0,1:T(8,128)}, u32[]{:S(2)}) %copy-start) | copy-done | bytes 65560
  2.1 0.0 copy-start.1
  2.1 0.7 copy-done.1
  2.8 0.0 copy-start.2
  2.8 0.7 copy-done.2
  3.5 0.0 copy-start.3
  3.5 0.7 copy-done.3
  4.2 0.0 copy-start.4
  4.2 0.7 copy-done.4
  4.9 0.0 copy-start.5
  4.9 0.7 copy-done.5
  5.5 0.0 copy-start.6
  5.5 0.7 copy-done.6
  6.2 0.0 copy-start.7
  6.2 0.7 copy-done.7
  6.8 62.7 %main_step.1 = (f32[128,128,256]{2,1,0:T(8,128)S(1)}, f32[64,16,256]{2,1,0:T(8,128)S(1)}, f32[128,256]{1,0:T(8,128)S(1)}) custom-call(s32[1]{0:T(128)S(6)} %copy.12.count, f32[3,32]{1,0:T(4,128)S(1)} %copy-done.2, f32[32]{0:T(128)S(1)} %copy-done.4, f32[32]{0:T(128)S(1)} %copy-done.5, f32[32]{0:T(128)S(1)} %copy-done.6, f32[32]{0:T(128)S(1)} %copy-done.7, ...), custom_call_target="tpu_custom_call" | custom-call | tf_op jit(solution)/shard_map/main_step/pallas_call | solution.py:511
  69.5 7.2 %emit_step.1 = (f32[128,128,256]{2,1,0:T(8,128)}, f32[128,256]{1,0:T(8,128)}) custom-call(f32[3,32]{1,0:T(4,128)S(1)} %copy-done.2, f32[32]{0:T(128)S(1)} %copy-done.4, f32[32]{0:T(128)S(1)} %copy-done.5, f32[128,128,256]{2,1,0:T(8,128)S(1)} %get-tuple-element.7.xv, f32[64,16,256]{2,1,0:T(8,128)S(1)} %get-tuple-element.8.inflow, ...), custom_call_target="tpu_custom_call" | custom-call | tf_op jit(solution)/shard_map/emit_step/pallas_call | solution.py:600
Async XLA Ops:
  1.3 0.8 %copy-start = (s32[1024,16]{0,1:T(8,128)S(1)}, s32[1024,16]{0,1:T(8,128)}, u32[]{:S(2)}) copy-start(s32[1024,16]{0,1:T(8,128)} %param.19) | copy-start | bytes 196612
  2.1 0.7 copy-start.1
  2.8 0.7 copy-start.2
  3.5 0.7 copy-start.3
  4.2 0.7 copy-start.4
  4.9 0.7 copy-start.5
  5.5 0.7 copy-start.6
  6.2 0.7 copy-start.7

commit v2 on v1

v2 whole, which is shorter than its diff:
```python
import functools

import jax
import jax.numpy as jnp
from jax import lax
from jax.experimental import pallas as pl
from jax.experimental.pallas import tpu as pltpu
from jax.sharding import PartitionSpec as P

MESH = pl.DeviceIdType.MESH
F32 = jnp.float32
BF16 = jnp.bfloat16
SUB, LANE = 8, 128
MIB = 1 << 20


def whole(space=pltpu.VMEM):
    return pl.BlockSpec(memory_space=space)


def in_hbm(*arrays):
    return tuple(pltpu.with_memory_space_constraint(a, pltpu.HBM) for a in arrays)


def squash(energy):
    return energy / (1.0 + 0.3 * jnp.abs(energy))


def send(src, dst, ssem, rsem, axis, target):
    return pltpu.make_async_remote_copy(
        src_ref=src,
        dst_ref=dst,
        send_sem=ssem,
        recv_sem=rsem,
        device_id={axis: target},
        device_id_type=MESH,
    )


class Reduction:
    def __init__(self, acc, slots, part, total, sems, n):
        self.acc, self.slots, self.part, self.total = acc, slots, part, total
        self.sems, self.n = sems, n
        self.me = lax.axis_index("mode")
        self.rows = acc.shape[0] // n

    def chunk(self, i):
        return pl.ds(pl.multiple_of(i * self.rows, self.rows), self.rows)

    def outward(self, off):
        target = lax.rem(self.me + off, self.n)
        return send(
            self.acc.at[self.chunk(target)], self.slots.at[off],
            self.sems.at[0, off], self.sems.at[1, off], "mode", target,
        )

    def spread(self, off):
        target = lax.rem(self.me + off, self.n)
        return send(
            self.part, self.total.at[self.chunk(self.me)],
            self.sems.at[2, off], self.sems.at[3, off], "mode", target,
        )

    def start(self):
        for off in range(1, self.n):
            self.outward(off).start()

    def combine(self, finish):
        for off in range(1, self.n):
            self.outward(off).wait_recv()
        value = self.acc[self.chunk(self.me), :]
        for off in range(1, self.n):
            value = value + self.slots[off]
        self.part[...] = finish(value)
        for off in range(1, self.n):
            self.spread(off).start()
        self.total[self.chunk(self.me), :] = self.part[...]

    def finish(self):
        for off in range(1, self.n):
            source = lax.rem(self.me + self.n - off, self.n)
            send(
                self.part, self.total.at[self.chunk(source)],
                self.sems.at[2, off], self.sems.at[3, off], "mode", source,
            ).wait_recv()
        for off in range(1, self.n):
            self.outward(off).wait_send()
            self.spread(off).wait_send()


def split(value):
    high = value.astype(BF16)
    return high, (value - high.astype(F32)).astype(BF16)


def splat(value):
    return jnp.full((SUB, LANE), value, F32)


def tiles(rows, width):
    return [(r, c) for r in range(0, rows, SUB) for c in range(0, width, LANE)]


def dot(a, b):
    return jnp.dot(a, b, preferred_element_type=F32)


def fine_dot(a, b):
    a_high, a_low = split(a)
    b_high, b_low = split(b)
    return dot(a_high, b_high) + (dot(a_high, b_low) + dot(a_low, b_high))


def turned_dot(a, b):
    contract = (((1,), (1,)), ((), ()))
    high, low = split(a)
    return lax.dot_general(high, b, contract, preferred_element_type=F32) + lax.dot_general(
        low, b, contract, preferred_element_type=F32
    )


def iota(shape, axis):
    return lax.broadcasted_iota(jnp.int32, shape, axis)


def copies(pairs, sem):
    return [pltpu.make_async_copy(src, dst, sem.at[i]) for i, (src, dst) in enumerate(pairs)]


def main_kernel(
    n, ns, planes,
    count, dir_cos_in, velocity_in, rate_in, spectrum_in, weight_in, heat_in, cells_in, reflect_in,
    x,
    xv, picked, equil, summed, smooth, live, marks,
    dir_cos, velocity, rate, spectrum, weight, dir_row, velocity_row, rate_row, spectrum_row,
    heat, cells, reflect,
    lo, hi, first, last, acc, slots1, part1, acc2, slots2, part2,
    held, block, lift, on_row, response, psem, lsem, hsem, sems1, sems2, ssem, rsem,
):
    me, sp = lax.axis_index("mode"), lax.axis_index("space")
    pairs, total_rows, width = xv.shape
    rows = total_rows // planes
    modes = velocity.shape[1]
    dirs = pairs // modes
    half = dirs // 2
    quiet = half * modes
    ups = reflect.shape[0]
    pairs_total = pairs * n
    rough = cells.shape[1]
    piece = quiet // 4
    batch = min(16, modes)
    per_dir = modes // batch
    order = [d for d in range(1, dirs, 2)] + [d for d in range(0, dirs, 2)]
    chunks = [(d, b) for d in order for b in range(per_dir)]

    fetched = copies((
        (cells_in, cells), (weight_in, weight), (dir_cos_in, dir_cos), (velocity_in, velocity),
        (rate_in, rate), (spectrum_in, spectrum), (dir_cos_in, dir_row),
        (velocity_in, velocity_row), (rate_in, rate_row), (spectrum_in, spectrum_row),
        (heat_in, heat), (reflect_in, reflect),
    ), psem)
    for copy in fetched:
        copy.start()

    def load(i):
        d, b = chunks[i]
        where = pl.ds(d * modes + b * batch, batch)
        return pltpu.make_async_copy(x.at[where], xv.at[where], lsem.at[i])

    for i in range(len(chunks)):
        load(i).start()

    def place_of(index):
        return jnp.where(lax.rem(index, 2) == 0, index // 2, n - 1 - index // 2)

    def index_of(place):
        place = lax.rem(place + n, n)
        return jnp.where(place < n // 2, 2 * place, 2 * (n - 1 - place) + 1)

    place = place_of(me)
    ends = (index_of(place + 1), index_of(place - 1))

    barrier = pltpu.get_barrier_semaphore()
    for off in range(1, n):
        pl.semaphore_signal(
            barrier, inc=1, device_id={"mode": lax.rem(me + off, n)}, device_id_type=MESH
        )

    @pl.when(sp > 0)
    def _():
        pl.semaphore_signal(barrier, inc=1, device_id={"space": sp - 1}, device_id_type=MESH)

    @pl.when(sp < ns - 1)
    def _():
        pl.semaphore_signal(barrier, inc=1, device_id={"space": sp + 1}, device_id_type=MESH)

    @pl.when(sp == 0)
    def _():
        lo[...] = jnp.zeros_like(lo)

    @pl.when(sp == ns - 1)
    def _():
        hi[...] = jnp.zeros_like(hi)

    acc[...] = jnp.zeros_like(acc)
    acc2[...] = jnp.zeros_like(acc2)
    for copy in fetched:
        copy.wait()
    marks[...] = jnp.where(iota((width, rough), 0) == lax.rem(cells[...], width), 1.0, 0.0).astype(
        BF16
    )
    on_row[...] = jnp.where(iota((rows, rough), 0) == cells[...] // width, 1.0, 0.0)
    low = jnp.where(sp > 0, 1, 0)
    high = jnp.where(sp < ns - 1, 1, 0)
    pl.semaphore_wait(barrier, n - 1 + low + high)

    def down_copy(i):
        d, b = chunks[i]
        where = pl.ds(d * modes + b * batch, batch)
        return send(
            first.at[where], hi.at[where], hsem.at[0, i], hsem.at[1, i], "space",
            lax.rem(sp + ns - 1, ns),
        )

    def up_copy(i):
        d, b = chunks[i]
        where = pl.ds(d * modes + b * batch, batch)
        return send(
            last.at[where], lo.at[where], hsem.at[2, i], hsem.at[3, i], "space",
            lax.rem(sp + 1, ns),
        )

    def halo_wait(i):
        @pl.when(sp > 0)
        def _():
            down_copy(i).wait_send()
            up_copy(i).wait_recv()

        @pl.when(sp < ns - 1)
        def _():
            up_copy(i).wait_send()
            down_copy(i).wait_recv()

    def take(i):
        d, b = chunks[i]
        base = d * modes + b * batch
        load(i).wait()

        def edges(t, carry):
            p = base + t
            for z in range(planes):
                first[p, pl.ds(z, 1), :] = xv[p, pl.ds(z * rows, 1), :]
                last[p, pl.ds(z, 1), :] = xv[p, pl.ds((z + 1) * rows - 1, 1), :]
            return carry

        lax.fori_loop(0, batch, edges, 0)

        @pl.when(sp > 0)
        def _():
            down_copy(i).start()

        @pl.when(sp < ns - 1)
        def _():
            up_copy(i).start()

        w = weight[0, me * dirs + d]

        def add_rows(r, carry):
            here = pl.ds(pl.multiple_of(r * SUB, SUB), SUB)
            value = xv[base, here, :]
            for t in range(1, batch):
                value = value + xv[base + t, here, :]
            acc[here, :] += w * value
            return carry

        lax.fori_loop(0, total_rows // SUB, add_rows, 0)

    row, lane = iota((SUB, LANE), 0), iota((SUB, LANE), 1)
    places = tiles(rows, width)
    last_row, last_col = rows - SUB, width - LANE

    def factors(d, m):
        s = me * dirs + d
        v = velocity[0, m]
        turn = v * jnp.abs(dir_cos[2, s])
        inv = 1.0 / splat(1.0 + rate[0, m] + turn)
        return v * jnp.abs(dir_cos[0, s]), v * jnp.abs(dir_cos[1, s]), turn, inv

    halo_done = set()

    def sweep(d, start, stop):
        for i, (dd, b) in enumerate(chunks):
            if dd == d and b * batch < stop and start < (b + 1) * batch and i not in halo_done:
                halo_done.add(i)
                halo_wait(i)
        s = me * dirs + d
        w = weight[0, s]
        low_x, low_y = splat(dir_cos[0, s]) >= 0.0, splat(dir_cos[1, s]) >= 0.0
        shift_x = jnp.where(dir_cos[0, s] >= 0.0, 1, SUB - 1)
        shift_y = jnp.where(dir_cos[1, s] >= 0.0, 1, LANE - 1)
        head_x, tail_x = low_x & (row == 0), ~low_x & (row == SUB - 1)
        head_y, tail_y = low_y & (lane == 0), ~low_y & (lane == LANE - 1)
        wide = 2

        def some(g, carry):
            sets, before = [], []
            for t in range(wide):
                m = start + g * wide + t
                vx, vy, turn, inv = factors(d, m)
                ky = inv * vy
                sets.append((
                    d * modes + m, inv * (1.0 - vx - vy), inv * vx, inv * turn,
                    ky, jnp.where(head_y, 0.0, ky), jnp.where(tail_y, 0.0, ky),
                ))
                if d % 2 == 0:
                    before.append({
                        (r, c): smooth[pl.ds(r, SUB), pl.ds(c, LANE)]
                        * xv[(d + 1) * modes + m, pl.ds(r, SUB), pl.ds(c, LANE)]
                        for r, c in places
                    })
                else:
                    before.append(None)
            for z in range(planes) if d % 2 == 0 else reversed(range(planes)):
                sums = {}
                for t in range(wide):
                    p, k0, kx, kp, ky, ky_head, ky_tail = sets[t]
                    own = {
                        (r, c): xv[p, pl.ds(z * rows + r, SUB), pl.ds(c, LANE)] for r, c in places
                    }
                    side = {at: pltpu.roll(own[at], shift_x, 0) for at in places}
                    along = {at: pltpu.roll(own[at], shift_y, 1) for at in places}
                    now = {}
                    for r, c in places:
                        cols = pl.ds(c, LANE)
                        if r == 0:
                            under = jnp.broadcast_to(lo[p, pl.ds(z, 1), cols], (SUB, LANE))
                        else:
                            under = side[r - SUB, c]
                        if r == last_row:
                            over = jnp.broadcast_to(hi[p, pl.ds(z, 1), cols], (SUB, LANE))
                        else:
                            over = side[r + SUB, c]
                        one = jnp.where(head_x, under, jnp.where(tail_x, over, side[r, c]))
                        two = along[r, c]
                        if c > 0:
                            two = jnp.where(head_y, along[r, c - LANE], two)
                        if c < last_col:
                            two = jnp.where(tail_y, along[r, c + LANE], two)
                        gain = ky
                        if c == 0:
                            gain = ky_head
                        if c == last_col:
                            gain = ky_tail if c else jnp.where(tail_y, 0.0, ky_head)
                        value = k0 * own[r, c] + kx * one + gain * two
                        if before[t] is not None:
                            value = value + kp * before[t][r, c]
                        now[r, c] = value
                        xv[p, pl.ds(z * rows + r, SUB), cols] = value
                        sums[r, c] = sums[r, c] + value if t else value
                    before[t] = now
                for r, c in places:
                    acc2[pl.ds(z * rows + r, SUB), pl.ds(c, LANE)] += w * sums[r, c]
            return carry

        lax.fori_loop(0, (stop - start) // wide, some, 0)

    def settle(h, start, stop):
        wide = 2
        up, down = 2 * h, 2 * h + 1

        def some(g, carry):
            sets, values = [], []
            for t in range(wide):
                m = start + g * wide + t
                _, _, turn, inv = factors(up, m)
                sets.append((m, inv * turn, inv * (rate[0, m] * spectrum[0, m])))
                values.append({
                    (r, c): heat[pl.ds(r, SUB), pl.ds(c, LANE)] * spectrum[0, m] for r, c in places
                })
            for d, z in [(down, z) for z in reversed(range(planes))] + [
                (up, z) for z in range(planes)
            ]:
                for r, c in places:
                    here, cols = pl.ds(z * rows + r, SUB), pl.ds(c, LANE)
                    level = equil[here, cols]
                    for t in range(wide):
                        m, kp, ks = sets[t]
                        value = values[t][r, c]
                        if d == up and z == 0:
                            value = value * smooth[pl.ds(r, SUB), cols]
                        value = kp * value + ks * level
                        values[t][r, c] = value
                        xv[d * modes + m, here, cols] += value
            return carry

        lax.fori_loop(0, (stop - start) // wide, some, 0)

    def rows_of(way, part):
        return (2 * way + part) * piece

    def pair_of(q):
        return (2 * (q // modes) + 1) * modes + q % modes

    def at_slots(values):
        k = values.shape[0]
        high, low = split(values.reshape(k * rows, width))
        column = marks[...]
        got = dot(high, column) + dot(low, column)
        return jnp.sum(got.reshape(k, rows, rough) * on_row[...][None], axis=1)

    def gather(q):
        held[place, pl.ds(q, piece), :] = at_slots(
            xv[pl.ds(pair_of(q), piece), pl.ds(0, rows), :]
        )

    def slot_of(way, step):
        return lax.rem(place + n + (-step if way == 0 else step), n)

    def copy_of(way, part, step):
        at = held.at[slot_of(way, step), pl.ds(rows_of(way, part), piece)]
        return send(at, at, ssem.at[way, part, step], rsem.at[way, part, step], "mode", ends[way])

    def arrival(way, part, step):
        at = held.at[slot_of(way, step + 1), pl.ds(rows_of(way, part), piece)]
        return send(at, at, ssem.at[way, part, step], rsem.at[way, part, step], "mode", ends[way])

    def choose(way, step):
        slot = slot_of(way, step)
        owner = index_of(slot)
        q0 = rows_of(way, 0)
        block[...] = (
            held[slot, pl.ds(q0, 2 * piece), :]
            + lift[pl.ds(pl.multiple_of(owner * quiet + q0, SUB), 2 * piece), :]
        )
        j, m0 = owner * half + q0 // modes, q0 % modes

        def one(k, carry):
            hit = reflect[pl.ds(k, 1), :] == j
            for q in range(0, 2 * piece, SUB):
                here = pl.ds(pl.multiple_of(k * modes + m0 + q, SUB), SUB)
                picked[here, :] = jnp.where(hit, block[pl.ds(q, SUB), :], picked[here, :])
            return carry

        lax.fori_loop(0, ups, one, 0)

    def prepare():
        size, lanes = ups * modes, response.shape[1]
        which = iota((size, 1), 0)
        modal = iota((size, modes), 1) == lax.rem(which, modes)
        angle = iota((size, 2 * ups), 1) == 2 * (which // modes) + 1

        def spread(mask, values):
            return jnp.sum(jnp.where(mask, values, 0.0), axis=1, keepdims=True)

        v, e = spread(modal, velocity_row[...]), spread(modal, rate_row[...])
        f = spread(modal, spectrum_row[...])
        turn = v * spread(angle, jnp.abs(dir_row[pl.ds(2, 1), :]))
        inv = 1.0 / (1.0 + e + turn)
        kp, power = turn * inv, inv * (e * f)
        at = iota((size, lanes), 1)
        out = jnp.zeros((size, lanes), F32)
        for z in range(planes):
            out = jnp.where(at == z, power, out)
            power = power * kp
        power = f * kp
        for z in range(planes - 1):
            power = power * kp
        response[...] = jnp.where(at == planes, power, out)

    def raise_all():
        lanes = response.shape[1]
        levels = at_slots(equil[...].reshape(planes, rows, width))
        face = at_slots(heat[...].reshape(1, rows, width))
        spare = jnp.zeros((lanes - planes - 1, rough), F32)
        sources = jnp.concatenate([levels, face, spare], axis=0)
        lift[...] = fine_dot(response[...], sources)

    def find_rough():
        live[...] = jnp.where(iota((rows, rough), 1) < count[0], on_row[...], 0.0)
        rough_at = lax.dot_general(
            live[...].astype(BF16), marks[...], (((1,), (1,)), ((), ())), preferred_element_type=F32
        )
        smooth[...] = jnp.where(rough_at > 0.5, 0.0, 0.9)

    opening = Reduction(acc, slots1, part1, equil, sems1, n)
    closing = Reduction(acc2, slots2, part2, summed, sems2, n)
    n_down = half * per_dir

    def launch(way, part):
        q = rows_of(way, part)
        sweep(2 * (q // modes) + 1, q % modes, q % modes + piece)
        gather(q)
        copy_of(way, part, 0).start()

    for i in range(n_down):
        take(i)
    find_rough()
    prepare()
    for way in range(2):
        launch(way, 0)
    for i in range(n_down, len(chunks)):
        take(i)
    opening.start()
    for way in range(2):
        launch(way, 1)

    def middle():
        opening.combine(lambda value: squash(value * (1.0 / pairs_total)))

    def third():
        opening.finish()
        raise_all()

    tasks = []
    slices = [(h, m) for h in range(half) for m in range(0, modes, SUB)]
    for i, (h, m) in enumerate(slices):
        tasks.append(functools.partial(sweep, 2 * h, m, m + SUB))
        if i == 1:
            tasks.append(middle)
    tasks.append(closing.start)
    tasks.append(third)
    for i, (h, m) in enumerate(slices):
        tasks.append(functools.partial(settle, h, m, m + SUB))
        if i == len(slices) - 3:
            tasks.append(lambda: closing.combine(lambda value: value))
    picked[...] = jnp.zeros_like(picked)
    total = len(tasks) + 2 * n
    events = 4 * (n - 1)
    for way in range(2):
        tasks.append(functools.partial(choose, way, 0))
    done, seen = 0, 0
    for step in range(1, n):
        for part in range(2):
            for way in range(2):
                arrival(way, part, step - 1).wait_recv()
                if step < n - 1:
                    copy_of(way, part, step).start()
                if part == 1:
                    tasks.append(functools.partial(choose, way, step))
                seen += 1
                while tasks and done * events < total * seen:
                    tasks.pop(0)()
                    done += 1
    for task in tasks:
        task()
    closing.finish()
    for step in range(n - 1):
        for part in range(2):
            for way in range(2):
                copy_of(way, part, step).wait_send()


def main_step(scalars, count, heat, cells, reflect, x, n, ns, planes):
    pairs, total_rows, width = x.shape
    rows = total_rows // planes
    modes = scalars[1].shape[1]
    quiet = pairs // 2
    rough = cells.shape[1]
    every = reflect.shape[0] * modes
    n_chunks = (pairs // modes) * (modes // min(16, modes))
    flat = (total_rows, width)
    part = (total_rows // n, width)
    halo = pltpu.VMEM((pairs, planes, width), F32)
    lanes = -(-(planes + 1) // 16) * 16
    return pl.pallas_call(
        functools.partial(main_kernel, n, ns, planes),
        out_shape=(
            jax.ShapeDtypeStruct(x.shape, F32),
            jax.ShapeDtypeStruct((every, rough), F32),
            jax.ShapeDtypeStruct(flat, F32),
            jax.ShapeDtypeStruct(flat, F32),
            jax.ShapeDtypeStruct((rows, width), F32),
            jax.ShapeDtypeStruct((rows, rough), F32),
            jax.ShapeDtypeStruct((width, rough), BF16),
        ),
        in_specs=[whole(pltpu.SMEM)] + [whole(pltpu.HBM)] * 9,
        out_specs=(whole(),) * 7,
        scratch_shapes=[
            *(pltpu.SMEM(a.shape, a.dtype) for a in scalars),
            *(pltpu.VMEM(a.shape, a.dtype) for a in (*scalars[:4], heat, cells, reflect)),
            halo, halo, halo, halo,
            pltpu.VMEM(flat, F32),
            pltpu.VMEM((n, *part), F32),
            pltpu.VMEM(part, F32),
            pltpu.VMEM(flat, F32),
            pltpu.VMEM((n, *part), F32),
            pltpu.VMEM(part, F32),
            pltpu.VMEM((n, quiet, rough), F32),
            pltpu.VMEM((quiet // 2, rough), F32),
            pltpu.VMEM((every, rough), F32),
            pltpu.VMEM((rows, rough), F32),
            pltpu.VMEM((every, lanes), F32),
            pltpu.SemaphoreType.DMA((12,)),
            pltpu.SemaphoreType.DMA((n_chunks,)),
            pltpu.SemaphoreType.DMA((4, n_chunks)),
            pltpu.SemaphoreType.DMA((4, n)),
            pltpu.SemaphoreType.DMA((4, n)),
            pltpu.SemaphoreType.DMA((2, 2, n - 1)),
            pltpu.SemaphoreType.DMA((2, 2, n - 1)),
        ],
        compiler_params=pltpu.CompilerParams(
            collective_id=0, has_side_effects=True, vmem_limit_bytes=28 * MIB
        ),
        name="main_step",
    )(count, *in_hbm(*scalars, heat, cells, reflect, x))


def emit_kernel(
    planes, pairs_total, dir_cos_in, velocity_in, rate_in, spectrum_in, weight_in, heat_in,
    xv, picked, equil, summed, smooth, live, marks,
    out, energy,
    dir_cos, velocity, rate, dir_row, velocity_row, rate_row, spectrum_row, weight_row, heat,
    rising, inflow, gains, moments, psem, sem,
):
    pairs, total_rows, width = xv.shape
    rows = total_rows // planes
    modes = velocity.shape[1]
    dirs = pairs // modes
    half = dirs // 2
    every, rough = picked.shape
    batch = min(8, modes)
    me = lax.axis_index("mode")
    places = tiles(rows, width)

    def whole_dir(d):
        where = pl.ds(d * modes, modes)
        return pltpu.make_async_copy(xv.at[where], out.at[where], sem.at[d, 0])

    def piece(d, b):
        return pltpu.make_async_copy(
            rising.at[pl.ds(d // 2 * modes + b * batch, batch)],
            out.at[pl.ds(d * modes + b * batch, batch)], sem.at[d, b],
        )

    fetched = copies((
        (dir_cos_in, dir_cos), (velocity_in, velocity), (rate_in, rate), (dir_cos_in, dir_row),
        (velocity_in, velocity_row), (rate_in, rate_row), (spectrum_in, spectrum_row),
        (weight_in, weight_row), (heat_in, heat),
    ), psem)
    for copy in fetched:
        copy.start()
    for d in range(1, dirs, 2):
        whole_dir(d).start()
    for copy in fetched:
        copy.wait()

    group = min(16, modes)
    for d in range(0, dirs, 2):
        cz = jnp.abs(dir_cos[2, me * dirs + d])
        for g in range(modes // group):
            first = pl.multiple_of((me * half + d // 2) * modes + g * group, group)
            spread = picked[pl.ds(first, group), :][:, None, :] * live[...][None]
            put = turned_dot(spread.reshape(group * rows, rough), marks[...])
            inflow[...] = 0.9 * put.reshape(group, rows, width)
            for b in range(g * group // batch, (g + 1) * group // batch):
                def one(i, carry):
                    m = b * batch + i
                    turn = velocity[0, m] * cz
                    ratio = splat(turn) / splat(1.0 + rate[0, m] + turn)
                    for r, c in places:
                        cols = pl.ds(c, LANE)
                        value = inflow[m - g * group, pl.ds(r, SUB), cols]
                        for z in range(planes):
                            here = pl.ds(z * rows + r, SUB)
                            value = ratio * value
                            rising[d // 2 * modes + m, here, cols] = (
                                xv[d * modes + m, here, cols] + value
                            )
                    return carry

                lax.fori_loop(0, batch, one, 0)
                piece(d, b).start()

    n_dirs = weight_row.shape[1]

    def column(values):
        size = values.shape[1]
        same = iota((size, size), 0) == iota((size, size), 1)
        return jnp.sum(jnp.where(same, values, 0.0), axis=1, keepdims=True)

    which = iota((1, every), 1)

    def spread_over(values, index):
        size = values.shape[1]
        mask = iota((size, every), 0) == index
        return jnp.sum(jnp.where(mask, column(values), 0.0), axis=0, keepdims=True)

    modal, angle = lax.rem(which, modes), 2 * (which // modes)
    v, e = spread_over(velocity_row[...], modal), spread_over(rate_row[...], modal)
    f = spread_over(spectrum_row[...], modal)
    turn = v * spread_over(jnp.abs(dir_row[pl.ds(2, 1), :]), angle)
    w_up, w_down = spread_over(weight_row[...], angle), spread_over(weight_row[...], angle + 1)
    inv = 1.0 / (1.0 + e + turn)
    kp, ks = turn * inv, inv * (e * f)
    top = 2 * planes + 2
    power = jnp.ones_like(kp)
    for q in range(top):
        if 1 <= q <= planes:
            gains[pl.ds(q - 1, 1), :] = 0.9 * w_up * power
        for i, scale in enumerate((w_up * ks, w_down * ks, w_up * f, w_down * f)):
            total = jnp.sum(scale * power, axis=1, keepdims=True)
            moments[i, pl.ds(q, 1), :] = jnp.broadcast_to(total, (1, LANE))
        power = power * kp
    at_slot = fine_dot(gains[...], picked[...])
    spread = at_slot[:, None, :] * live[...][None]
    rough_part = turned_dot(spread.reshape(total_rows, rough), marks[...])

    def moment(i, q):
        return jnp.broadcast_to(moments[i, pl.ds(q, 1), :], (SUB, LANE))

    for r, c in places:
        cols = pl.ds(c, LANE)
        levels = [equil[pl.ds(z * rows + r, SUB), cols] for z in range(planes)]
        face = heat[pl.ds(r, SUB), cols]
        plain = smooth[pl.ds(r, SUB), cols]
        for z in range(planes):
            here = pl.ds(z * rows + r, SUB)
            value = summed[here, cols] + rough_part[z * rows + r : z * rows + r + SUB, c : c + LANE]
            value = value + moment(3, planes - z) * face
            turned = moment(2, z + 1 + planes) * face
            for y in range(planes):
                if y <= z:
                    value = value + moment(0, z - y) * levels[y]
                if y >= z:
                    value = value + moment(1, y - z) * levels[y]
                turned = turned + moment(0, z + 1 + y) * levels[y]
            energy[here, cols] = (value + plain * turned) * (1.0 / pairs_total)
    for d in range(dirs):
        if d % 2:
            whole_dir(d).wait()
        else:
            for b in range(modes // batch):
                piece(d, b).wait()


def emit_step(planes, pairs_total, scalars, heat, parts):
    xv, picked = parts[:2]
    pairs, total_rows, width = xv.shape
    modes = scalars[1].shape[1]
    rows = total_rows // planes
    return pl.pallas_call(
        functools.partial(emit_kernel, planes, pairs_total),
        out_shape=(
            jax.ShapeDtypeStruct(xv.shape, F32),
            jax.ShapeDtypeStruct((total_rows, width), F32),
        ),
        in_specs=[whole(pltpu.HBM)] * 6 + [whole()] * len(parts),
        out_specs=(whole(pltpu.HBM), whole()),
        scratch_shapes=[
            *(pltpu.SMEM(a.shape, a.dtype) for a in scalars[:3]),
            *(pltpu.VMEM(a.shape, a.dtype) for a in (*scalars, heat)),
            pltpu.VMEM((pairs // 2, total_rows, width), F32),
            pltpu.VMEM((min(16, modes), rows, width), F32),
            pltpu.VMEM((planes, picked.shape[0]), F32),
            pltpu.VMEM((4, -(-(2 * planes + 2) // SUB) * SUB, LANE), F32),
            pltpu.SemaphoreType.DMA((9,)),
            pltpu.SemaphoreType.DMA((pairs // modes, modes // min(8, modes))),
        ],
        compiler_params=pltpu.CompilerParams(vmem_limit_bytes=28 * MIB),
        name="emit_step",
    )(*in_hbm(*scalars, heat), *parts)


def per_device(
    n, ns, intensity, dir_cos, velocity, rate, spectrum, weight, heat, rough_cells, rough_count,
    rough_map,
):
    pairs, planes, rows, width = intensity.shape
    x = intensity.reshape(pairs, planes * rows, width)
    scalars = (dir_cos, velocity[None], rate[None], spectrum[None], weight[None])
    parts = main_step(scalars, rough_count, heat, rough_cells[None], rough_map.T, x, n, ns, planes)
    fresh, energy = emit_step(planes, pairs * n, scalars, heat, parts)
    return fresh.reshape(intensity.shape), energy.reshape(planes, rows, width)


def solution(mesh):
    n, ns = mesh.shape["mode"], mesh.shape["space"]
    in_specs = (
        P("mode", None, "space", None),
        P(),
        P(),
        P(),
        P(),
        P(),
        P("space", None),
        P("space"),
        P("space"),
        P("space", None),
    )
    out_specs = (P("mode", None, "space", None), P(None, "space", None))
    return jax.shard_map(
        functools.partial(per_device, n, ns),
        mesh=mesh,
        in_specs=in_specs,
        out_specs=out_specs,
        check_vma=False,
    )
```

time: 77 us -> 61.9 us (0.80)
  Pallas kernels: 69.9 us -> 60.1 us
  local copies, waits for them, and re-layouts: 5.54 us -> 0 us
    pallas_call x1, Pallas kernels: 62.7 us -> 52.5 us  [main_step(): pl.pallas_call(functools.partial(main_kernel, n, ns, planes), out_shape=(...]
    unnamed x16 -> x0, local copies, waits for them, and re-layouts: 5.54 us -> none
where the time goes in v2:
time: 61.9 us; the launch traced here: 61.4 us
  Pallas kernels  60.1 us (97%)
  between operations  1.28 us (2%)
    pallas_call x1, Pallas kernels, main_step(): pl.pallas_call(functools.partial(main_kernel, n, ns, planes), out_shape=(...  52.5 us
    pallas_call x1, Pallas kernels, emit_step(): pl.pallas_call(functools.partial(emit_kernel, planes, pairs_total), out_s...  7.57 us

profile of v2, /device:TPU:0, one launch (start us, length us, event | category | flops | bytes accessed | tf_op | source)
XLA Modules:
  0.0 61.4 jit_solution(14794620756536738119)
XLA Ops:
  1.3 52.5 %main_step.1 = (f32[128,128,256]{2,1,0:T(8,128)S(1)}, f32[512,1024]{1,0:T(8,128)S(1)}, f32[128,256]{1,0:T(8,128)S(1)}, f32[128,256]{1,0:T(8,128)S(1)}, f32[16,25...) custom-call(s32[1]{0:T(128)S(6)} %copy.12.count, f32[3,32]{1,0:T(4,128)} %dir_cos_in.3, ...), custom_call_target="tpu_custom_call" | custom-call | tf_op jit(solution)/shard_map/main_step/pallas_call | solution.py:565
  53.8 7.6 %emit_step.1 = (f32[128,128,256]{2,1,0:T(8,128)}, f32[128,256]{1,0:T(8,128)}) custom-call(f32[3,32]{1,0:T(4,128)} %dir_cos_in.3, f32[1,32]{1,0:T(1,128)} %bitcast.13, f32[1,32]{1,0:T(1,128)} %bitcast.15, f32[1,32]{1,0:T(1,128)} %bitcast.17, f32[1,32]{1,0:T(1,128)} %bitcast.19, f32[16,256]{1,0:T(8,128)} %heat_in.3, ...), custom_call_target="tpu_custom_call" | custom-call | tf_op jit(solution)/shard_map/emit_step/pallas_call | solution.py:741

commit v3 on v2

--- a/solution.py
+++ b/solution.py
@@ -131,11 +131,12 @@
     n, ns, planes,
     count, dir_cos_in, velocity_in, rate_in, spectrum_in, weight_in, heat_in, cells_in, reflect_in,
     x,
-    xv, picked, equil, summed, smooth, live, marks,
+    xv, returned, glow, equil, summed, smooth, live, marks,
     dir_cos, velocity, rate, spectrum, weight, dir_row, velocity_row, rate_row, spectrum_row,
-    heat, cells, reflect,
+    weight_row, heat, cells, reflect,
     lo, hi, first, last, acc, slots1, part1, acc2, slots2, part2,
-    held, block, lift, on_row, response, psem, lsem, hsem, sems1, sems2, ssem, rsem,
+    outbox, inbox, wanted, picked, shine, on_row, response, gains,
+    psem, lsem, hsem, sems1, sems2, gone, come, back_gone, back_come,
 ):
     me, sp = lax.axis_index("mode"), lax.axis_index("space")
     pairs, total_rows, width = xv.shape
@@ -147,6 +148,7 @@
     ups = reflect.shape[0]
     pairs_total = pairs * n
     rough = cells.shape[1]
+    share = rough // n
     piece = quiet // 4
     batch = min(16, modes)
     per_dir = modes // batch
@@ -157,7 +159,7 @@
         (cells_in, cells), (weight_in, weight), (dir_cos_in, dir_cos), (velocity_in, velocity),
         (rate_in, rate), (spectrum_in, spectrum), (dir_cos_in, dir_row),
         (velocity_in, velocity_row), (rate_in, rate_row), (spectrum_in, spectrum_row),
-        (heat_in, heat), (reflect_in, reflect),
+        (weight_in, weight_row), (heat_in, heat), (reflect_in, reflect),
     ), psem)
     for copy in fetched:
         copy.start()
@@ -169,16 +171,6 @@
 
     for i in range(len(chunks)):
         load(i).start()
-
-    def place_of(index):
-        return jnp.where(lax.rem(index, 2) == 0, index // 2, n - 1 - index // 2)
-
-    def index_of(place):
-        place = lax.rem(place + n, n)
-        return jnp.where(place < n // 2, 2 * place, 2 * (n - 1 - place) + 1)
-
-    place = place_of(me)
-    ends = (index_of(place + 1), index_of(place - 1))
 
     barrier = pltpu.get_barrier_semaphore()
     for off in range(1, n):
@@ -395,9 +387,6 @@
 
         lax.fori_loop(0, (stop - start) // wide, some, 0)
 
-    def rows_of(way, part):
-        return (2 * way + part) * piece
-
     def pair_of(q):
         return (2 * (q // modes) + 1) * modes + q % modes
 
@@ -408,40 +397,94 @@
         got = dot(high, column) + dot(low, column)
         return jnp.sum(got.reshape(k, rows, rough) * on_row[...][None], axis=1)
 
-    def gather(q):
-        held[place, pl.ds(q, piece), :] = at_slots(
-            xv[pl.ds(pair_of(q), piece), pl.ds(0, rows), :]
+    def shares(values):
+        return [values[:, i * share : (i + 1) * share] for i in range(n)]
+
+    def outward(part, off):
+        target = lax.rem(me + off, n)
+        here = pl.ds(part * piece, piece)
+        return send(
+            outbox.at[target, here], inbox.at[me, here], gone.at[part, off], come.at[part, off],
+            "mode", target,
         )
 
-    def slot_of(way, step):
-        return lax.rem(place + n + (-step if way == 0 else step), n)
-
-    def copy_of(way, part, step):
-        at = held.at[slot_of(way, step), pl.ds(rows_of(way, part), piece)]
-        return send(at, at, ssem.at[way, part, step], rsem.at[way, part, step], "mode", ends[way])
-
-    def arrival(way, part, step):
-        at = held.at[slot_of(way, step + 1), pl.ds(rows_of(way, part), piece)]
-        return send(at, at, ssem.at[way, part, step], rsem.at[way, part, step], "mode", ends[way])
-
-    def choose(way, step):
-        slot = slot_of(way, step)
-        owner = index_of(slot)
-        q0 = rows_of(way, 0)
-        block[...] = (
-            held[slot, pl.ds(q0, 2 * piece), :]
-            + lift[pl.ds(pl.multiple_of(owner * quiet + q0, SUB), 2 * piece), :]
+    def arrival(part, off):
+        source = lax.rem(me + n - off, n)
+        here = pl.ds(part * piece, piece)
+        return send(
+            outbox.at[source, here], inbox.at[source, here], gone.at[part, off],
+            come.at[part, off], "mode", source,
         )
-        j, m0 = owner * half + q0 // modes, q0 % modes
+
+    def homeward(off):
+        target = lax.rem(me + off, n)
+        mine = pl.ds(pl.multiple_of(target * quiet, quiet), quiet)
+        return [
+            send(
+                picked.at[mine], returned.at[me], back_gone.at[0, off], back_come.at[0, off],
+                "mode", target,
+            ),
+            send(shine, glow.at[me], back_gone.at[1, off], back_come.at[1, off], "mode", target),
+        ]
+
+    def return_of(off):
+        source = lax.rem(me + n - off, n)
+        mine = pl.ds(pl.multiple_of(me * quiet, quiet), quiet)
+        return [
+            send(
+                picked.at[mine], returned.at[source], back_gone.at[0, off], back_come.at[0, off],
+                "mode", source,
+            ),
+            send(
+                shine, glow.at[source], back_gone.at[1, off], back_come.at[1, off], "mode", source
+            ),
+        ]
+
+    def launch(part):
+        q = part * piece
+        sweep(2 * (q // modes) + 1, q % modes, q % modes + piece)
+        got = at_slots(xv[pl.ds(pair_of(q), piece), pl.ds(0, rows), :])
+        for i, value in enumerate(shares(got)):
+            outbox[i, pl.ds(q, piece), :] = value
+        for off in range(1, n):
+            outward(part, off).start()
+        inbox[me, pl.ds(q, piece), :] = outbox[me, pl.ds(q, piece), :]
+
+    def own_share(values):
+        total = jnp.zeros((values.shape[0], share), values.dtype)
+        for i, value in enumerate(shares(values)):
+            total = jnp.where(me == i, value, total)
+        return total
+
+    def choose():
+        for part in range(4):
+            for off in range(1, n):
+                arrival(part, off).wait_recv()
+        lanes = response.shape[1]
+        levels = at_slots(equil[...].reshape(planes, rows, width))
+        face = at_slots(heat[...].reshape(1, rows, width))
+        spare = jnp.zeros((lanes - planes - 1, rough), F32)
+        sources = own_share(jnp.concatenate([levels, face, spare], axis=0))
+        lift = fine_dot(response[...], sources)
+        inbox[...] += lift.reshape(n, quiet, share)
+        wanted[...] = own_share(reflect[...])
 
         def one(k, carry):
-            hit = reflect[pl.ds(k, 1), :] == j
-            for q in range(0, 2 * piece, SUB):
-                here = pl.ds(pl.multiple_of(k * modes + m0 + q, SUB), SUB)
-                picked[here, :] = jnp.where(hit, block[pl.ds(q, SUB), :], picked[here, :])
+            want = wanted[pl.ds(k, 1), :]
+            value = None
+            for j in range(ups):
+                source = inbox[j // half, pl.ds((j % half) * modes, modes), :]
+                value = source if j == 0 else jnp.where(want == j, source, value)
+            picked[pl.ds(pl.multiple_of(k * modes, modes), modes), :] = value
             return carry
 
         lax.fori_loop(0, ups, one, 0)
+        shine[...] = fine_dot(gains[...], picked[...])
+        for off in range(1, n):
+            for copy in homeward(off):
+                copy.start()
+        returned[me] = picked[pl.ds(pl.multiple_of(me * quiet, quiet), quiet), :]
+        glow[me] = shine[...]
 
     def prepare():
         size, lanes = ups * modes, response.shape[1]
@@ -467,13 +510,23 @@
             power = power * kp
         response[...] = jnp.where(at == planes, power, out)
 
-    def raise_all():
-        lanes = response.shape[1]
-        levels = at_slots(equil[...].reshape(planes, rows, width))
-        face = at_slots(heat[...].reshape(1, rows, width))
-        spare = jnp.zeros((lanes - planes - 1, rough), F32)
-        sources = jnp.concatenate([levels, face, spare], axis=0)
-        lift[...] = fine_dot(response[...], sources)
+        which = iota((1, size), 1)
+
+        def along(values, index):
+            length = values.shape[1]
+            same = iota((length, length), 0) == iota((length, length), 1)
+            column = jnp.sum(jnp.where(same, values, 0.0), axis=1, keepdims=True)
+            mask = iota((length, size), 0) == index
+            return jnp.sum(jnp.where(mask, column, 0.0), axis=0, keepdims=True)
+
+        modal, angle = lax.rem(which, modes), 2 * (which // modes)
+        v, e = along(velocity_row[...], modal), along(rate_row[...], modal)
+        turn = v * along(jnp.abs(dir_row[pl.ds(2, 1), :]), angle)
+        kp = turn / (1.0 + e + turn)
+        power = 0.9 * along(weight_row[...], angle)
+        for z in range(planes):
+            power = power * kp
+            gains[pl.ds(z, 1), :] = power
 
     def find_rough():
         live[...] = jnp.where(iota((rows, rough), 1) < count[0], on_row[...], 0.0)
@@ -486,68 +539,43 @@
     closing = Reduction(acc2, slots2, part2, summed, sems2, n)
     n_down = half * per_dir
 
-    def launch(way, part):
-        q = rows_of(way, part)
-        sweep(2 * (q // modes) + 1, q % modes, q % modes + piece)
-        gather(q)
-        copy_of(way, part, 0).start()
-
     for i in range(n_down):
         take(i)
-    find_rough()
-    prepare()
-    for way in range(2):
-        launch(way, 0)
+    for part in range(2):
+        launch(part)
     for i in range(n_down, len(chunks)):
         take(i)
     opening.start()
-    for way in range(2):
-        launch(way, 1)
-
-    def middle():
-        opening.combine(lambda value: squash(value * (1.0 / pairs_total)))
-
-    def third():
-        opening.finish()
-        raise_all()
-
-    tasks = []
+    for part in range(2, 4):
+        launch(part)
+    find_rough()
     slices = [(h, m) for h in range(half) for m in range(0, modes, SUB)]
+    early = min(2, len(slices) - 1)
+    for h, m in slices[:early]:
+        sweep(2 * h, m, m + SUB)
+    opening.combine(lambda value: squash(value * (1.0 / pairs_total)))
+    prepare()
+    middle = min(6, len(slices) - 1)
+    for h, m in slices[early:middle]:
+        sweep(2 * h, m, m + SUB)
+    opening.finish()
+    choose()
+    for h, m in slices[middle:]:
+        sweep(2 * h, m, m + SUB)
+    closing.start()
     for i, (h, m) in enumerate(slices):
-        tasks.append(functools.partial(sweep, 2 * h, m, m + SUB))
-        if i == 1:
-            tasks.append(middle)
-    tasks.append(closing.start)
-    tasks.append(third)
-    for i, (h, m) in enumerate(slices):
-        tasks.append(functools.partial(settle, h, m, m + SUB))
-        if i == len(slices) - 3:
-            tasks.append(lambda: closing.combine(lambda value: value))
-    picked[...] = jnp.zeros_like(picked)
-    total = len(tasks) + 2 * n
-    events = 4 * (n - 1)
-    for way in range(2):
-        tasks.append(functools.partial(choose, way, 0))
-    done, seen = 0, 0
-    for step in range(1, n):
-        for part in range(2):
-            for way in range(2):
-                arrival(way, part, step - 1).wait_recv()
-                if step < n - 1:
-                    copy_of(way, part, step).start()
-                if part == 1:
-                    tasks.append(functools.partial(choose, way, step))
-                seen += 1
-                while tasks and done * events < total * seen:
-                    tasks.pop(0)()
-                    done += 1
-    for task in tasks:
-        task()
+        settle(h, m, m + SUB)
+        if i == len(slices) // 2:
+            closing.combine(lambda value: value)
     closing.finish()
-    for step in range(n - 1):
-        for part in range(2):
-            for way in range(2):
-                copy_of(way, part, step).wait_send()
+    for off in range(1, n):
+        for copy in return_of(off):
+            copy.wait_recv()
+    for off in range(1, n):
+        for part in range(4):
+            outward(part, off).wait_send()
+        for copy in homeward(off):
+            copy.wait_send()
 
 
 def main_step(scalars, count, heat, cells, reflect, x, n, ns, planes):
@@ -557,6 +585,7 @@
     quiet = pairs // 2
     rough = cells.shape[1]
     every = reflect.shape[0] * modes
+    share = rough // n
     n_chunks = (pairs // modes) * (modes // min(16, modes))
     flat = (total_rows, width)
     part = (total_rows // n, width)
@@ -566,7 +595,8 @@
         functools.partial(main_kernel, n, ns, planes),
         out_shape=(
             jax.ShapeDtypeStruct(x.shape, F32),
-            jax.ShapeDtypeStruct((every, rough), F32),
+            jax.ShapeDtypeStruct((n, quiet, share), F32),
+            jax.ShapeDtypeStruct((n, planes, share), F32),
             jax.ShapeDtypeStruct(flat, F32),
             jax.ShapeDtypeStruct(flat, F32),
             jax.ShapeDtypeStruct((rows, width), F32),
@@ -574,10 +604,10 @@
             jax.ShapeDtypeStruct((width, rough), BF16),
         ),
         in_specs=[whole(pltpu.SMEM)] + [whole(pltpu.HBM)] * 9,
-        out_specs=(whole(),) * 7,
+        out_specs=(whole(),) * 8,
         scratch_shapes=[
             *(pltpu.SMEM(a.shape, a.dtype) for a in scalars),
-            *(pltpu.VMEM(a.shape, a.dtype) for a in (*scalars[:4], heat, cells, reflect)),
+            *(pltpu.VMEM(a.shape, a.dtype) for a in (*scalars, heat, cells, reflect)),
             halo, halo, halo, halo,
             pltpu.VMEM(flat, F32),
             pltpu.VMEM((n, *part), F32),
@@ -585,18 +615,23 @@
             pltpu.VMEM(flat, F32),
             pltpu.VMEM((n, *part), F32),
             pltpu.VMEM(part, F32),
-            pltpu.VMEM((n, quiet, rough), F32),
-            pltpu.VMEM((quiet // 2, rough), F32),
-            pltpu.VMEM((every, rough), F32),
+            pltpu.VMEM((n, quiet, share), F32),
+            pltpu.VMEM((n, quiet, share), F32),
+            pltpu.VMEM((reflect.shape[0], share), jnp.int32),
+            pltpu.VMEM((every, share), F32),
+            pltpu.VMEM((planes, share), F32),
             pltpu.VMEM((rows, rough), F32),
             pltpu.VMEM((every, lanes), F32),
-            pltpu.SemaphoreType.DMA((12,)),
+            pltpu.VMEM((planes, every), F32),
+            pltpu.SemaphoreType.DMA((13,)),
             pltpu.SemaphoreType.DMA((n_chunks,)),
             pltpu.SemaphoreType.DMA((4, n_chunks)),
             pltpu.SemaphoreType.DMA((4, n)),
             pltpu.SemaphoreType.DMA((4, n)),
-            pltpu.SemaphoreType.DMA((2, 2, n - 1)),
-            pltpu.SemaphoreType.DMA((2, 2, n - 1)),
+            pltpu.SemaphoreType.DMA((4, n)),
+            pltpu.SemaphoreType.DMA((4, n)),
+            pltpu.SemaphoreType.DMA((2, n)),
+            pltpu.SemaphoreType.DMA((2, n)),
         ],
         compiler_params=pltpu.CompilerParams(
             collective_id=0, has_side_effects=True, vmem_limit_bytes=28 * MIB
@@ -607,17 +642,19 @@
 
 def emit_kernel(
     planes, pairs_total, dir_cos_in, velocity_in, rate_in, spectrum_in, weight_in, heat_in,
-    xv, picked, equil, summed, smooth, live, marks,
+    xv, returned, glow, equil, summed, smooth, live, marks,
     out, energy,
     dir_cos, velocity, rate, dir_row, velocity_row, rate_row, spectrum_row, weight_row, heat,
-    rising, inflow, gains, moments, psem, sem,
+    rising, inflow, moments, psem, sem,
 ):
     pairs, total_rows, width = xv.shape
     rows = total_rows // planes
     modes = velocity.shape[1]
     dirs = pairs // modes
     half = dirs // 2
-    every, rough = picked.shape
+    rough = live.shape[1]
+    n = returned.shape[0]
+    every = n * half * modes
     batch = min(8, modes)
     me = lax.axis_index("mode")
     places = tiles(rows, width)
@@ -648,8 +685,9 @@
     for d in range(0, dirs, 2):
         cz = jnp.abs(dir_cos[2, me * dirs + d])
         for g in range(modes // group):
-            first = pl.multiple_of((me * half + d // 2) * modes + g * group, group)
-            spread = picked[pl.ds(first, group), :][:, None, :] * live[...][None]
+            first = pl.ds(d // 2 * modes + g * group, group)
+            own = jnp.concatenate([returned[i, first, :] for i in range(n)], axis=1)
+            spread = own[:, None, :] * live[...][None]
             put = turned_dot(spread.reshape(group * rows, rough), marks[...])
             inflow[...] = 0.9 * put.reshape(group, rows, width)
             for b in range(g * group // batch, (g + 1) * group // batch):
@@ -695,13 +733,11 @@
     top = 2 * planes + 2
     power = jnp.ones_like(kp)
     for q in range(top):
-        if 1 <= q <= planes:
-            gains[pl.ds(q - 1, 1), :] = 0.9 * w_up * power
         for i, scale in enumerate((w_up * ks, w_down * ks, w_up * f, w_down * f)):
             total = jnp.sum(scale * power, axis=1, keepdims=True)
             moments[i, pl.ds(q, 1), :] = jnp.broadcast_to(total, (1, LANE))
         power = power * kp
-    at_slot = fine_dot(gains[...], picked[...])
+    at_slot = jnp.concatenate([glow[i] for i in range(n)], axis=1)
     spread = at_slot[:, None, :] * live[...][None]
     rough_part = turned_dot(spread.reshape(total_rows, rough), marks[...])
 
@@ -734,7 +770,7 @@
 
 
 def emit_step(planes, pairs_total, scalars, heat, parts):
-    xv, picked = parts[:2]
+    xv = parts[0]
     pairs, total_rows, width = xv.shape
     modes = scalars[1].shape[1]
     rows = total_rows // planes
@@ -751,7 +787,6 @@
             *(pltpu.VMEM(a.shape, a.dtype) for a in (*scalars, heat)),
             pltpu.VMEM((pairs // 2, total_rows, width), F32),
             pltpu.VMEM((min(16, modes), rows, width), F32),
-            pltpu.VMEM((planes, picked.shape[0]), F32),
             pltpu.VMEM((4, -(-(2 * planes + 2) // SUB) * SUB, LANE), F32),
             pltpu.SemaphoreType.DMA((9,)),
             pltpu.SemaphoreType.DMA((pairs // modes, modes // min(8, modes))),

time: 61.9 us -> 55.2 us (0.89)
  Pallas kernels: 60.1 us -> 53.6 us
    pallas_call x1, Pallas kernels: 52.5 us -> 46.4 us  [main_step(): pl.pallas_call(functools.partial(main_kernel, n, ns, planes), out_shape=(...]
where the time goes in v3:
time: 55.2 us; the launch traced here: 54.9 us
  Pallas kernels  53.6 us (97%)
  between operations  1.28 us (2%)
    pallas_call x1, Pallas kernels, main_step(): pl.pallas_call(functools.partial(main_kernel, n, ns, planes), out_shape=(...  46.4 us
    pallas_call x1, Pallas kernels, emit_step(): pl.pallas_call(functools.partial(emit_kernel, planes, pairs_total), out_s...  7.25 us

profile of v3, /device:TPU:0, one launch (start us, length us, event | category | flops | bytes accessed | tf_op | source)
XLA Modules:
  0.0 54.9 jit_solution(8620020551787350429)
XLA Ops:
  1.3 46.4 %main_step.1 = (f32[128,128,256]{2,1,0:T(8,128)S(1)}, f32[8,64,128]{2,1,0:T(8,128)S(1)}, f32[8,8,128]{2,1,0:T(8,128)S(1)}, f32[128,256]{1,0:T(8,128)S(1)}, f32[1...) custom-call(s32[1]{0:T(128)S(6)} %copy.12.count, ...), custom_call_target="tpu_custom_call" | custom-call | tf_op jit(solution)/shard_map/main_step/pallas_call | solution.py:594
  47.7 7.2 %emit_step.1 = (f32[128,128,256]{2,1,0:T(8,128)}, f32[128,256]{1,0:T(8,128)}) custom-call(f32[3,32]{1,0:T(4,128)} %dir_cos_in.3, f32[1,32]{1,0:T(1,128)} %bitcast.13, f32[1,32]{1,0:T(1,128)} %bitcast.15, f32[1,32]{1,0:T(1,128)} %bitcast.17, f32[1,32]{1,0:T(1,128)} %bitcast.19, f32[16,256]{1,0:T(8,128)} %heat_in.3, ...), custom_call_target="tpu_custom_call" | custom-call | tf_op jit(solution)/shard_map/emit_step/pallas_call | solution.py:777

commit v4 on v3

--- a/solution.py
+++ b/solution.py
@@ -135,6 +135,7 @@
     dir_cos, velocity, rate, spectrum, weight, dir_row, velocity_row, rate_row, spectrum_row,
     weight_row, heat, cells, reflect,
     lo, hi, first, last, acc, slots1, part1, acc2, slots2, part2,
+    table, plain, swift, bottom, edge,
     outbox, inbox, wanted, picked, shine, on_row, response, gains,
     psem, lsem, hsem, sems1, sems2, gone, come, back_gone, back_come,
 ):
@@ -210,7 +211,7 @@
         d, b = chunks[i]
         where = pl.ds(d * modes + b * batch, batch)
         return send(
-            first.at[where], hi.at[where], hsem.at[0, i], hsem.at[1, i], "space",
+            first.at[:, :, where], hi.at[:, :, where], hsem.at[0, i], hsem.at[1, i], "space",
             lax.rem(sp + ns - 1, ns),
         )
 
@@ -218,7 +219,7 @@
         d, b = chunks[i]
         where = pl.ds(d * modes + b * batch, batch)
         return send(
-            last.at[where], lo.at[where], hsem.at[2, i], hsem.at[3, i], "space",
+            last.at[:, :, where], lo.at[:, :, where], hsem.at[2, i], hsem.at[3, i], "space",
             lax.rem(sp + 1, ns),
         )
 
@@ -241,8 +242,10 @@
         def edges(t, carry):
             p = base + t
             for z in range(planes):
-                first[p, pl.ds(z, 1), :] = xv[p, pl.ds(z * rows, 1), :]
-                last[p, pl.ds(z, 1), :] = xv[p, pl.ds((z + 1) * rows - 1, 1), :]
+                for k in range(width // LANE):
+                    cols = pl.ds(k * LANE, LANE)
+                    first[k, z, pl.ds(p, 1), :] = xv[p, pl.ds(z * rows, 1), cols]
+                    last[k, z, pl.ds(p, 1), :] = xv[p, pl.ds((z + 1) * rows - 1, 1), cols]
             return carry
 
         lax.fori_loop(0, batch, edges, 0)
@@ -255,65 +258,219 @@
         def _():
             up_copy(i).start()
 
-        w = weight[0, me * dirs + d]
-
-        def add_rows(r, carry):
-            here = pl.ds(pl.multiple_of(r * SUB, SUB), SUB)
-            value = xv[base, here, :]
-            for t in range(1, batch):
-                value = value + xv[base + t, here, :]
-            acc[here, :] += w * value
-            return carry
-
-        lax.fori_loop(0, total_rows // SUB, add_rows, 0)
+        survey(d, b * batch, b * batch + batch)
 
     row, lane = iota((SUB, LANE), 0), iota((SUB, LANE), 1)
     places = tiles(rows, width)
     last_row, last_col = rows - SUB, width - LANE
 
-    def factors(d, m):
+    def gain(d, kind, m):
+        return jnp.broadcast_to(table[d, kind, pl.ds(m, 1), :], (SUB, LANE))
+
+    def cosines(d):
+        return [jnp.abs(dir_cos[axis, me * dirs + d]) for axis in range(3)]
+
+    def signs(d):
         s = me * dirs + d
-        v = velocity[0, m]
-        turn = v * jnp.abs(dir_cos[2, s])
-        inv = 1.0 / splat(1.0 + rate[0, m] + turn)
-        return v * jnp.abs(dir_cos[0, s]), v * jnp.abs(dir_cos[1, s]), turn, inv
+        low_x, low_y = splat(dir_cos[0, s]) >= 0.0, splat(dir_cos[1, s]) >= 0.0
+        return (
+            jnp.where(dir_cos[0, s] >= 0.0, 1, SUB - 1),
+            jnp.where(dir_cos[1, s] >= 0.0, 1, LANE - 1),
+            low_x & (row == 0), ~low_x & (row == SUB - 1),
+            low_y & (lane == 0), ~low_y & (lane == LANE - 1),
+        )
+
+    def level_order(d):
+        return list(range(planes)) if d % 2 == 0 else list(reversed(range(planes)))
+
+    def tabulate():
+        same = iota((modes, modes), 0) == iota((modes, modes), 1)
+
+        def column(values):
+            return jnp.sum(jnp.where(same, values, 0.0), axis=1, keepdims=True)
+
+        v, e, f = column(velocity_row[...]), column(rate_row[...]), column(spectrum_row[...])
+        for d in range(dirs):
+            inv = 1.0 / (1.0 + e + v * cosines(d)[2])
+            for kind, value in enumerate((inv, inv * v, inv * (e * f))):
+                table[d, kind] = jnp.broadcast_to(value, (modes, LANE))
+
+    def survey(d, start, stop):
+        cz = cosines(d)[2]
+        w = weight[0, me * dirs + d]
+        levels = level_order(d)
+        for r, c in places:
+            cols = pl.ds(c, LANE)
+
+            def one(t, carry):
+                sums = [list(part) for part in carry]
+                for m in (start + 2 * t, start + 2 * t + 1):
+                    inv, fast = gain(d, 0, m), gain(d, 1, m)
+                    kp = fast * cz
+                    u = None
+                    for z in levels:
+                        value = xv[d * modes + m, pl.ds(z * rows + r, SUB), cols]
+                        u = value if u is None else value + kp * u
+                        sums[0][z] = sums[0][z] + value
+                        sums[1][z] = sums[1][z] + inv * u
+                        sums[2][z] = sums[2][z] + fast * u
+                    if d % 2:
+                        bottom[d // 2 * modes + m, pl.ds(r, SUB), cols] = u
+                return tuple(tuple(part) for part in sums)
+
+            zero = tuple(jnp.zeros((SUB, LANE), F32) for _ in range(planes))
+            sums = lax.fori_loop(0, (stop - start) // 2, one, (zero, zero, zero))
+            for z in range(planes):
+                here = pl.ds(z * rows + r, SUB)
+                acc[here, cols] += w * sums[0][z]
+                if start == 0:
+                    plain[d, here, cols] = sums[1][z]
+                    swift[d, here, cols] = sums[2][z]
+                else:
+                    plain[d, here, cols] += sums[1][z]
+                    swift[d, here, cols] += sums[2][z]
+
+    def neighbours(own, kinds):
+        shift_x, shift_y, head_x, tail_x, head_y, tail_y = kinds
+        side = {at: pltpu.roll(own[at], shift_x, 0) for at in places}
+        along = {at: pltpu.roll(own[at], shift_y, 1) for at in places}
+        ones, twos = {}, {}
+        for r, c in places:
+            under = side[r - SUB, c] if r else 0.0
+            over = side[r + SUB, c] if r < last_row else 0.0
+            ones[r, c] = jnp.where(head_x, under, jnp.where(tail_x, over, side[r, c]))
+            left = along[r, c - LANE] if c else 0.0
+            right = along[r, c + LANE] if c < last_col else 0.0
+            twos[r, c] = jnp.where(head_y, left, jnp.where(tail_y, right, along[r, c]))
+        return ones, twos
+
+    def edge_rows(d):
+        s = me * dirs + d
+        w = weight[0, s]
+        cx, _, cz = cosines(d)
+        _, _, head_x, tail_x, _, _ = signs(d)
+        from_low = splat(dir_cos[0, s]) >= 0.0
+        for c in range(0, width, LANE):
+            cols = pl.ds(c, LANE)
+            totals = [None] * planes
+            for m in range(0, modes, SUB):
+                fast = table[d, 1, pl.ds(m, SUB), :]
+                kp, kx = fast * cz, fast * cx
+                here = pl.ds(d * modes + m, SUB)
+                u = None
+                for z in level_order(d):
+                    value = jnp.where(from_low, lo[c // LANE, z, here], hi[c // LANE, z, here])
+                    u = value if u is None else value + kp * u
+                    now = kx * u
+                    totals[z] = now if totals[z] is None else totals[z] + now
+                if d % 2:
+                    edge[c // LANE, pl.ds(d // 2 * modes + m, SUB), :] = now
+            for z in range(planes):
+                line = jnp.broadcast_to(jnp.sum(totals[z], axis=0, keepdims=True), (SUB, LANE))
+                top, end = pl.ds(z * rows, SUB), pl.ds(z * rows + last_row, SUB)
+                acc2[top, cols] += jnp.where(head_x, w * line, 0.0)
+                acc2[end, cols] += jnp.where(tail_x, w * line, 0.0)
+
+    def ground(start, stop):
+        d = 2 * (start // modes) + 1
+        cx, cy, _ = cosines(d)
+        kinds = signs(d)
+        head_x, tail_x = kinds[2:4]
+
+        def one(t, carry):
+            q = start + t
+            m = start % modes + t
+            inv, fast = gain(d, 0, m), gain(d, 1, m)
+            kx, ky = fast * cx, fast * cy
+            k0 = inv - kx - ky
+            own = {(r, c): bottom[q, pl.ds(r, SUB), pl.ds(c, LANE)] for r, c in places}
+            ones, twos = neighbours(own, kinds)
+            for r, c in places:
+                value = k0 * own[r, c] + kx * ones[r, c] + ky * twos[r, c]
+                line = jnp.broadcast_to(edge[c // LANE, pl.ds(q, 1), :], (SUB, LANE))
+                if r == 0:
+                    value = value + jnp.where(head_x, line, 0.0)
+                if r == last_row:
+                    value = value + jnp.where(tail_x, line, 0.0)
+                bottom[q, pl.ds(r, SUB), pl.ds(c, LANE)] = value
+            return carry
+
+        lax.fori_loop(0, stop - start, one, 0)
+
+    def glide(h):
+        cz = cosines(2 * h)[2]
+        w = weight[0, me * dirs + 2 * h]
+        for r, c in places:
+            cols = pl.ds(c, LANE)
+
+            def one(t, carry):
+                sums = list(carry)
+                for m in (2 * t, 2 * t + 1):
+                    kp = gain(2 * h, 1, m) * cz
+                    value = bottom[h * modes + m, pl.ds(r, SUB), cols]
+                    for z in range(planes):
+                        value = kp * value
+                        sums[z] = sums[z] + value
+                return tuple(sums)
+
+            zero = tuple(jnp.zeros((SUB, LANE), F32) for _ in range(planes))
+            sums = lax.fori_loop(0, modes // 2, one, zero)
+            scale = w * smooth[pl.ds(r, SUB), cols]
+            for z in range(planes):
+                acc2[pl.ds(z * rows + r, SUB), cols] += scale * sums[z]
+
+    def tally(d):
+        cx, cy, _ = cosines(d)
+        w = weight[0, me * dirs + d]
+        kinds = signs(d)
+
+        def one(z, carry):
+            at = {
+                (r, c): (pl.ds(pl.multiple_of(z * rows, SUB) + r, SUB), pl.ds(c, LANE))
+                for r, c in places
+            }
+            own = {k: swift[(d, *at[k])] for k in places}
+            ones, twos = neighbours(own, kinds)
+            for k in places:
+                value = plain[(d, *at[k])] - (cx + cy) * own[k] + cx * ones[k] + cy * twos[k]
+                acc2[at[k]] += w * value
+            return carry
+
+        lax.fori_loop(0, planes, one, 0)
 
     halo_done = set()
 
-    def sweep(d, start, stop):
+    def halo_for(d, start, stop):
         for i, (dd, b) in enumerate(chunks):
             if dd == d and b * batch < stop and start < (b + 1) * batch and i not in halo_done:
                 halo_done.add(i)
                 halo_wait(i)
-        s = me * dirs + d
-        w = weight[0, s]
-        low_x, low_y = splat(dir_cos[0, s]) >= 0.0, splat(dir_cos[1, s]) >= 0.0
-        shift_x = jnp.where(dir_cos[0, s] >= 0.0, 1, SUB - 1)
-        shift_y = jnp.where(dir_cos[1, s] >= 0.0, 1, LANE - 1)
-        head_x, tail_x = low_x & (row == 0), ~low_x & (row == SUB - 1)
-        head_y, tail_y = low_y & (lane == 0), ~low_y & (lane == LANE - 1)
+
+    def sweep(d, start, stop):
+        halo_for(d, start, stop)
+        cx, cy, cz = cosines(d)
+        shift_x, shift_y, head_x, tail_x, head_y, tail_y = signs(d)
         wide = 2
 
         def some(g, carry):
             sets, before = [], []
             for t in range(wide):
                 m = start + g * wide + t
-                vx, vy, turn, inv = factors(d, m)
-                ky = inv * vy
+                inv, fast = gain(d, 0, m), gain(d, 1, m)
+                kx, ky = fast * cx, fast * cy
                 sets.append((
-                    d * modes + m, inv * (1.0 - vx - vy), inv * vx, inv * turn,
+                    d * modes + m, inv - kx - ky, kx, fast * cz,
                     ky, jnp.where(head_y, 0.0, ky), jnp.where(tail_y, 0.0, ky),
                 ))
                 if d % 2 == 0:
                     before.append({
                         (r, c): smooth[pl.ds(r, SUB), pl.ds(c, LANE)]
-                        * xv[(d + 1) * modes + m, pl.ds(r, SUB), pl.ds(c, LANE)]
+                        * bottom[d // 2 * modes + m, pl.ds(r, SUB), pl.ds(c, LANE)]
                         for r, c in places
                     })
                 else:
                     before.append(None)
             for z in range(planes) if d % 2 == 0 else reversed(range(planes)):
-                sums = {}
                 for t in range(wide):
                     p, k0, kx, kp, ky, ky_head, ky_tail = sets[t]
                     own = {
@@ -325,11 +482,11 @@
                     for r, c in places:
                         cols = pl.ds(c, LANE)
                         if r == 0:
-                            under = jnp.broadcast_to(lo[p, pl.ds(z, 1), cols], (SUB, LANE))
+                            under = jnp.broadcast_to(lo[c // LANE, z, pl.ds(p, 1), :], (SUB, LANE))
                         else:
                             under = side[r - SUB, c]
                         if r == last_row:
-                            over = jnp.broadcast_to(hi[p, pl.ds(z, 1), cols], (SUB, LANE))
+                            over = jnp.broadcast_to(hi[c // LANE, z, pl.ds(p, 1), :], (SUB, LANE))
                         else:
                             over = side[r + SUB, c]
                         one = jnp.where(head_x, under, jnp.where(tail_x, over, side[r, c]))
@@ -338,20 +495,17 @@
                             two = jnp.where(head_y, along[r, c - LANE], two)
                         if c < last_col:
                             two = jnp.where(tail_y, along[r, c + LANE], two)
-                        gain = ky
+                        weigh = ky
                         if c == 0:
-                            gain = ky_head
+                            weigh = ky_head
                         if c == last_col:
-                            gain = ky_tail if c else jnp.where(tail_y, 0.0, ky_head)
-                        value = k0 * own[r, c] + kx * one + gain * two
+                            weigh = ky_tail if c else jnp.where(tail_y, 0.0, ky_head)
+                        value = k0 * own[r, c] + kx * one + weigh * two
                         if before[t] is not None:
                             value = value + kp * before[t][r, c]
                         now[r, c] = value
                         xv[p, pl.ds(z * rows + r, SUB), cols] = value
-                        sums[r, c] = sums[r, c] + value if t else value
                     before[t] = now
-                for r, c in places:
-                    acc2[pl.ds(z * rows + r, SUB), pl.ds(c, LANE)] += w * sums[r, c]
             return carry
 
         lax.fori_loop(0, (stop - start) // wide, some, 0)
@@ -364,8 +518,7 @@
             sets, values = [], []
             for t in range(wide):
                 m = start + g * wide + t
-                _, _, turn, inv = factors(up, m)
-                sets.append((m, inv * turn, inv * (rate[0, m] * spectrum[0, m])))
+                sets.append((m, gain(up, 1, m) * cosines(up)[2], gain(up, 2, m)))
                 values.append({
                     (r, c): heat[pl.ds(r, SUB), pl.ds(c, LANE)] * spectrum[0, m] for r, c in places
                 })
@@ -387,9 +540,6 @@
 
         lax.fori_loop(0, (stop - start) // wide, some, 0)
 
-    def pair_of(q):
-        return (2 * (q // modes) + 1) * modes + q % modes
-
     def at_slots(values):
         k = values.shape[0]
         high, low = split(values.reshape(k * rows, width))
@@ -442,8 +592,8 @@
 
     def launch(part):
         q = part * piece
-        sweep(2 * (q // modes) + 1, q % modes, q % modes + piece)
-        got = at_slots(xv[pl.ds(pair_of(q), piece), pl.ds(0, rows), :])
+        ground(q, q + piece)
+        got = at_slots(bottom[pl.ds(q, piece)])
         for i, value in enumerate(shares(got)):
             outbox[i, pl.ds(q, piece), :] = value
         for off in range(1, n):
@@ -537,36 +687,40 @@
 
     opening = Reduction(acc, slots1, part1, equil, sems1, n)
     closing = Reduction(acc2, slots2, part2, summed, sems2, n)
-    n_down = half * per_dir
-
-    for i in range(n_down):
-        take(i)
-    for part in range(2):
-        launch(part)
-    for i in range(n_down, len(chunks)):
+
+    tabulate()
+    for i in range(len(chunks)):
         take(i)
     opening.start()
-    for part in range(2, 4):
+    for d in range(1, dirs, 2):
+        halo_for(d, 0, modes)
+        edge_rows(d)
+    for part in range(4):
         launch(part)
     find_rough()
-    slices = [(h, m) for h in range(half) for m in range(0, modes, SUB)]
-    early = min(2, len(slices) - 1)
-    for h, m in slices[:early]:
-        sweep(2 * h, m, m + SUB)
     opening.combine(lambda value: squash(value * (1.0 / pairs_total)))
+    for h in range(half):
+        glide(h)
+    for d in range(dirs):
+        tally(d)
+    for d in range(0, dirs, 2):
+        halo_for(d, 0, modes)
+        edge_rows(d)
+    closing.start()
     prepare()
-    middle = min(6, len(slices) - 1)
-    for h, m in slices[early:middle]:
-        sweep(2 * h, m, m + SUB)
+    slices = [(d, m) for d in range(dirs) for m in range(0, modes, SUB)]
+    cuts = [len(slices) * i // 8 for i in (0, 2, 5, 8)]
+    for d, m in slices[cuts[0] : cuts[1]]:
+        sweep(d, m, m + SUB)
     opening.finish()
     choose()
-    for h, m in slices[middle:]:
-        sweep(2 * h, m, m + SUB)
-    closing.start()
-    for i, (h, m) in enumerate(slices):
-        settle(h, m, m + SUB)
-        if i == len(slices) // 2:
-            closing.combine(lambda value: value)
+    for d, m in slices[cuts[1] : cuts[2]]:
+        sweep(d, m, m + SUB)
+    closing.combine(lambda value: value)
+    for d, m in slices[cuts[2] : cuts[3]]:
+        sweep(d, m, m + SUB)
+    for h in range(half):
+        settle(h, 0, modes)
     closing.finish()
     for off in range(1, n):
         for copy in return_of(off):
@@ -589,7 +743,7 @@
     n_chunks = (pairs // modes) * (modes // min(16, modes))
     flat = (total_rows, width)
     part = (total_rows // n, width)
-    halo = pltpu.VMEM((pairs, planes, width), F32)
+    halo = pltpu.VMEM((width // LANE, planes, pairs, LANE), F32)
     lanes = -(-(planes + 1) // 16) * 16
     return pl.pallas_call(
         functools.partial(main_kernel, n, ns, planes),
@@ -615,6 +769,11 @@
             pltpu.VMEM(flat, F32),
             pltpu.VMEM((n, *part), F32),
             pltpu.VMEM(part, F32),
+            pltpu.VMEM((pairs // modes, 3, modes, LANE), F32),
+            pltpu.VMEM((pairs // modes, *flat), F32),
+            pltpu.VMEM((pairs // modes, *flat), F32),
+            pltpu.VMEM((quiet, rows, width), F32),
+            pltpu.VMEM((width // LANE, quiet, LANE), F32),
             pltpu.VMEM((n, quiet, share), F32),
             pltpu.VMEM((n, quiet, share), F32),
             pltpu.VMEM((reflect.shape[0], share), jnp.int32),

time: 55.2 us -> 56.8 us (1.029)
  Pallas kernels: 53.6 us -> 55.3 us
    pallas_call x1, Pallas kernels: 46.4 us -> 48.1 us  [main_step(): pl.pallas_call(functools.partial(main_kernel, n, ns, planes), out_shape=(...]
where the time goes in v4:
time: 56.8 us; the launch traced here: 56.6 us
  Pallas kernels  55.3 us (97%)
  between operations  1.28 us (2%)
    pallas_call x1, Pallas kernels, main_step(): pl.pallas_call(functools.partial(main_kernel, n, ns, planes), out_shape=(...  48.1 us
    pallas_call x1, Pallas kernels, emit_step(): pl.pallas_call(functools.partial(emit_kernel, planes, pairs_total), out_s...  7.25 us

profile of v4, /device:TPU:0, one launch (start us, length us, event | category | flops | bytes accessed | tf_op | source)
XLA Modules:
  0.0 56.6 jit_solution(2224565909510774454)
XLA Ops:
  1.3 48.1 %main_step.1 = (f32[128,128,256]{2,1,0:T(8,128)S(1)}, f32[8,64,128]{2,1,0:T(8,128)S(1)}, f32[8,8,128]{2,1,0:T(8,128)S(1)}, f32[128,256]{1,0:T(8,128)S(1)}, f32[1...) custom-call(s32[1]{0:T(128)S(6)} %copy.12.count, ...), custom_call_target="tpu_custom_call" | custom-call | tf_op jit(solution)/shard_map/main_step/pallas_call | solution.py:748
  49.4 7.2 %emit_step.1 = (f32[128,128,256]{2,1,0:T(8,128)}, f32[128,256]{1,0:T(8,128)}) custom-call(f32[3,32]{1,0:T(4,128)} %dir_cos_in.3, f32[1,32]{1,0:T(1,128)} %bitcast.13, f32[1,32]{1,0:T(1,128)} %bitcast.15, f32[1,32]{1,0:T(1,128)} %bitcast.17, f32[1,32]{1,0:T(1,128)} %bitcast.19, f32[16,256]{1,0:T(8,128)} %heat_in.3, ...), custom_call_target="tpu_custom_call" | custom-call | tf_op jit(solution)/shard_map/emit_step/pallas_call | solution.py:936

commit v5 on v3

--- a/solution.py
+++ b/solution.py
@@ -135,11 +135,12 @@
     dir_cos, velocity, rate, spectrum, weight, dir_row, velocity_row, rate_row, spectrum_row,
     weight_row, heat, cells, reflect,
     lo, hi, first, last, acc, slots1, part1, acc2, slots2, part2,
-    outbox, inbox, wanted, picked, shine, on_row, response, gains,
+    table, outbox, inbox, wanted, picked, shine, on_row, response, gains,
     psem, lsem, hsem, sems1, sems2, gone, come, back_gone, back_come,
 ):
     me, sp = lax.axis_index("mode"), lax.axis_index("space")
-    pairs, total_rows, width = xv.shape
+    pairs, strips, total_rows, _ = xv.shape
+    width = strips * LANE
     rows = total_rows // planes
     modes = velocity.shape[1]
     dirs = pairs // modes
@@ -167,10 +168,16 @@
     def load(i):
         d, b = chunks[i]
         where = pl.ds(d * modes + b * batch, batch)
-        return pltpu.make_async_copy(x.at[where], xv.at[where], lsem.at[i])
+        return [
+            pltpu.make_async_copy(
+                x.at[where, :, pl.ds(k * LANE, LANE)], xv.at[where, k], lsem.at[k, i]
+            )
+            for k in range(strips)
+        ]
 
     for i in range(len(chunks)):
-        load(i).start()
+        for copy in load(i):
+            copy.start()
 
     barrier = pltpu.get_barrier_semaphore()
     for off in range(1, n):
@@ -202,10 +209,6 @@
         BF16
     )
     on_row[...] = jnp.where(iota((rows, rough), 0) == cells[...] // width, 1.0, 0.0)
-    low = jnp.where(sp > 0, 1, 0)
-    high = jnp.where(sp < ns - 1, 1, 0)
-    pl.semaphore_wait(barrier, n - 1 + low + high)
-
     def down_copy(i):
         d, b = chunks[i]
         where = pl.ds(d * modes + b * batch, batch)
@@ -233,16 +236,35 @@
             up_copy(i).wait_send()
             down_copy(i).wait_recv()
 
-    def take(i):
+    def add_up(i):
         d, b = chunks[i]
         base = d * modes + b * batch
-        load(i).wait()
+        for copy in load(i):
+            copy.wait()
+        w = weight[0, me * dirs + d]
+
+        def add_rows(r, carry):
+            here = pl.ds(pl.multiple_of(r * SUB, SUB), SUB)
+            for k in range(strips):
+                value = xv[base, k, here, :]
+                for t in range(1, batch):
+                    value = value + xv[base + t, k, here, :]
+                acc[here, pl.ds(k * LANE, LANE)] += w * value
+            return carry
+
+        lax.fori_loop(0, total_rows // SUB, add_rows, 0)
+
+    def share_edges(i):
+        d, b = chunks[i]
+        base = d * modes + b * batch
 
         def edges(t, carry):
             p = base + t
             for z in range(planes):
-                first[p, pl.ds(z, 1), :] = xv[p, pl.ds(z * rows, 1), :]
-                last[p, pl.ds(z, 1), :] = xv[p, pl.ds((z + 1) * rows - 1, 1), :]
+                for k in range(strips):
+                    cols = pl.ds(k * LANE, LANE)
+                    first[p, pl.ds(z, 1), cols] = xv[p, k, pl.ds(z * rows, 1), :]
+                    last[p, pl.ds(z, 1), cols] = xv[p, k, pl.ds((z + 1) * rows - 1, 1), :]
             return carry
 
         lax.fori_loop(0, batch, edges, 0)
@@ -255,28 +277,27 @@
         def _():
             up_copy(i).start()
 
-        w = weight[0, me * dirs + d]
-
-        def add_rows(r, carry):
-            here = pl.ds(pl.multiple_of(r * SUB, SUB), SUB)
-            value = xv[base, here, :]
-            for t in range(1, batch):
-                value = value + xv[base + t, here, :]
-            acc[here, :] += w * value
-            return carry
-
-        lax.fori_loop(0, total_rows // SUB, add_rows, 0)
-
     row, lane = iota((SUB, LANE), 0), iota((SUB, LANE), 1)
     places = tiles(rows, width)
     last_row, last_col = rows - SUB, width - LANE
 
-    def factors(d, m):
-        s = me * dirs + d
-        v = velocity[0, m]
-        turn = v * jnp.abs(dir_cos[2, s])
-        inv = 1.0 / splat(1.0 + rate[0, m] + turn)
-        return v * jnp.abs(dir_cos[0, s]), v * jnp.abs(dir_cos[1, s]), turn, inv
+    def gain(d, kind, m):
+        return jnp.broadcast_to(table[d, kind, pl.ds(m, 1), :], (SUB, LANE))
+
+    def cosines(d):
+        return [jnp.abs(dir_cos[axis, me * dirs + d]) for axis in range(3)]
+
+    def tabulate():
+        same = iota((modes, modes), 0) == iota((modes, modes), 1)
+
+        def column(values):
+            return jnp.sum(jnp.where(same, values, 0.0), axis=1, keepdims=True)
+
+        v, e, f = column(velocity_row[...]), column(rate_row[...]), column(spectrum_row[...])
+        for d in range(dirs):
+            inv = 1.0 / (1.0 + e + v * cosines(d)[2])
+            for kind, value in enumerate((inv, inv * v, inv * (e * f))):
+                table[d, kind] = jnp.broadcast_to(value, (modes, LANE))
 
     halo_done = set()
 
@@ -288,7 +309,9 @@
         s = me * dirs + d
         w = weight[0, s]
         low_x, low_y = splat(dir_cos[0, s]) >= 0.0, splat(dir_cos[1, s]) >= 0.0
+        cx, cy, cz = cosines(d)
         shift_x = jnp.where(dir_cos[0, s] >= 0.0, 1, SUB - 1)
+        step_x = jnp.where(dir_cos[0, s] >= 0.0, -1, 1)
         shift_y = jnp.where(dir_cos[1, s] >= 0.0, 1, LANE - 1)
         head_x, tail_x = low_x & (row == 0), ~low_x & (row == SUB - 1)
         head_y, tail_y = low_y & (lane == 0), ~low_y & (lane == LANE - 1)
@@ -298,16 +321,16 @@
             sets, before = [], []
             for t in range(wide):
                 m = start + g * wide + t
-                vx, vy, turn, inv = factors(d, m)
-                ky = inv * vy
+                inv, fast = gain(d, 0, m), gain(d, 1, m)
+                kx, ky = fast * cx, fast * cy
                 sets.append((
-                    d * modes + m, inv * (1.0 - vx - vy), inv * vx, inv * turn,
+                    d * modes + m, inv - kx - ky, kx, fast * cz,
                     ky, jnp.where(head_y, 0.0, ky), jnp.where(tail_y, 0.0, ky),
                 ))
                 if d % 2 == 0:
                     before.append({
                         (r, c): smooth[pl.ds(r, SUB), pl.ds(c, LANE)]
-                        * xv[(d + 1) * modes + m, pl.ds(r, SUB), pl.ds(c, LANE)]
+                        * xv[(d + 1) * modes + m, c // LANE, pl.ds(r, SUB), :]
                         for r, c in places
                     })
                 else:
@@ -317,37 +340,52 @@
                 for t in range(wide):
                     p, k0, kx, kp, ky, ky_head, ky_tail = sets[t]
                     own = {
-                        (r, c): xv[p, pl.ds(z * rows + r, SUB), pl.ds(c, LANE)] for r, c in places
+                        (r, c): xv[p, c // LANE, pl.ds(z * rows + r, SUB), :] for r, c in places
                     }
-                    side = {at: pltpu.roll(own[at], shift_x, 0) for at in places}
                     along = {at: pltpu.roll(own[at], shift_y, 1) for at in places}
-                    now = {}
+                    now, ones = {}, {}
+                    for r, c in places:
+                        k, at_row = c // LANE, z * rows + r
+                        under = over = None
+                        if r == 0:
+                            under = jnp.broadcast_to(
+                                lo[p, pl.ds(z, 1), pl.ds(c, LANE)], (SUB, LANE)
+                            )
+                        if r == last_row:
+                            over = jnp.broadcast_to(
+                                hi[p, pl.ds(z, 1), pl.ds(c, LANE)], (SUB, LANE)
+                            )
+                        if 0 < at_row < total_rows - SUB:
+                            one = xv[p, k, pl.ds(at_row + step_x, SUB), :]
+                        else:
+                            one = pltpu.roll(own[r, c], shift_x, 0)
+                            if under is None:
+                                under = pltpu.roll(own[r - SUB, c], 1, 0)
+                            if over is None:
+                                over = pltpu.roll(own[r + SUB, c], SUB - 1, 0)
+                        if under is not None:
+                            one = jnp.where(head_x, under, one)
+                        if over is not None:
+                            one = jnp.where(tail_x, over, one)
+                        ones[r, c] = one
                     for r, c in places:
                         cols = pl.ds(c, LANE)
-                        if r == 0:
-                            under = jnp.broadcast_to(lo[p, pl.ds(z, 1), cols], (SUB, LANE))
-                        else:
-                            under = side[r - SUB, c]
-                        if r == last_row:
-                            over = jnp.broadcast_to(hi[p, pl.ds(z, 1), cols], (SUB, LANE))
-                        else:
-                            over = side[r + SUB, c]
-                        one = jnp.where(head_x, under, jnp.where(tail_x, over, side[r, c]))
+                        one = ones[r, c]
                         two = along[r, c]
                         if c > 0:
                             two = jnp.where(head_y, along[r, c - LANE], two)
                         if c < last_col:
                             two = jnp.where(tail_y, along[r, c + LANE], two)
-                        gain = ky
+                        weigh = ky
                         if c == 0:
-                            gain = ky_head
+                            weigh = ky_head
                         if c == last_col:
-                            gain = ky_tail if c else jnp.where(tail_y, 0.0, ky_head)
-                        value = k0 * own[r, c] + kx * one + gain * two
+                            weigh = ky_tail if c else jnp.where(tail_y, 0.0, ky_head)
+                        value = k0 * own[r, c] + kx * one + weigh * two
                         if before[t] is not None:
                             value = value + kp * before[t][r, c]
                         now[r, c] = value
-                        xv[p, pl.ds(z * rows + r, SUB), cols] = value
+                        xv[p, c // LANE, pl.ds(z * rows + r, SUB), :] = value
                         sums[r, c] = sums[r, c] + value if t else value
                     before[t] = now
                 for r, c in places:
@@ -364,8 +402,7 @@
             sets, values = [], []
             for t in range(wide):
                 m = start + g * wide + t
-                _, _, turn, inv = factors(up, m)
-                sets.append((m, inv * turn, inv * (rate[0, m] * spectrum[0, m])))
+                sets.append((m, gain(up, 1, m) * cosines(up)[2], gain(up, 2, m)))
                 values.append({
                     (r, c): heat[pl.ds(r, SUB), pl.ds(c, LANE)] * spectrum[0, m] for r, c in places
                 })
@@ -382,7 +419,7 @@
                             value = value * smooth[pl.ds(r, SUB), cols]
                         value = kp * value + ks * level
                         values[t][r, c] = value
-                        xv[d * modes + m, here, cols] += value
+                        xv[d * modes + m, c // LANE, here, :] += value
             return carry
 
         lax.fori_loop(0, (stop - start) // wide, some, 0)
@@ -443,7 +480,8 @@
     def launch(part):
         q = part * piece
         sweep(2 * (q // modes) + 1, q % modes, q % modes + piece)
-        got = at_slots(xv[pl.ds(pair_of(q), piece), pl.ds(0, rows), :])
+        strip = [xv[pl.ds(pair_of(q), piece), k, pl.ds(0, rows), :] for k in range(strips)]
+        got = at_slots(jnp.concatenate(strip, axis=2))
         for i, value in enumerate(shares(got)):
             outbox[i, pl.ds(q, piece), :] = value
         for off in range(1, n):
@@ -537,27 +575,27 @@
 
     opening = Reduction(acc, slots1, part1, equil, sems1, n)
     closing = Reduction(acc2, slots2, part2, summed, sems2, n)
-    n_down = half * per_dir
-
-    for i in range(n_down):
-        take(i)
-    for part in range(2):
+
+    tabulate()
+    add_up(0)
+    low = jnp.where(sp > 0, 1, 0)
+    high = jnp.where(sp < ns - 1, 1, 0)
+    pl.semaphore_wait(barrier, n - 1 + low + high)
+    share_edges(0)
+    for i in range(1, len(chunks)):
+        add_up(i)
+        share_edges(i)
+    opening.start()
+    for part in range(4):
         launch(part)
-    for i in range(n_down, len(chunks)):
-        take(i)
-    opening.start()
-    for part in range(2, 4):
-        launch(part)
+        if part == 2:
+            opening.combine(lambda value: squash(value * (1.0 / pairs_total)))
     find_rough()
     slices = [(h, m) for h in range(half) for m in range(0, modes, SUB)]
-    early = min(2, len(slices) - 1)
-    for h, m in slices[:early]:
+    middle = len(slices) // 2
+    for h, m in slices[:middle]:
         sweep(2 * h, m, m + SUB)
-    opening.combine(lambda value: squash(value * (1.0 / pairs_total)))
     prepare()
-    middle = min(6, len(slices) - 1)
-    for h, m in slices[early:middle]:
-        sweep(2 * h, m, m + SUB)
     opening.finish()
     choose()
     for h, m in slices[middle:]:
@@ -565,9 +603,7 @@
     closing.start()
     for i, (h, m) in enumerate(slices):
         settle(h, m, m + SUB)
-        if i == len(slices) // 2:
-            closing.combine(lambda value: value)
-    closing.finish()
+    closing.combine(lambda value: value)
     for off in range(1, n):
         for copy in return_of(off):
             copy.wait_recv()
@@ -576,6 +612,7 @@
             outward(part, off).wait_send()
         for copy in homeward(off):
             copy.wait_send()
+    closing.finish()
 
 
 def main_step(scalars, count, heat, cells, reflect, x, n, ns, planes):
@@ -594,7 +631,7 @@
     return pl.pallas_call(
         functools.partial(main_kernel, n, ns, planes),
         out_shape=(
-            jax.ShapeDtypeStruct(x.shape, F32),
+            jax.ShapeDtypeStruct((pairs, width // LANE, total_rows, LANE), F32),
             jax.ShapeDtypeStruct((n, quiet, share), F32),
             jax.ShapeDtypeStruct((n, planes, share), F32),
             jax.ShapeDtypeStruct(flat, F32),
@@ -615,6 +652,7 @@
             pltpu.VMEM(flat, F32),
             pltpu.VMEM((n, *part), F32),
             pltpu.VMEM(part, F32),
+            pltpu.VMEM((pairs // modes, 3, modes, LANE), F32),
             pltpu.VMEM((n, quiet, share), F32),
             pltpu.VMEM((n, quiet, share), F32),
             pltpu.VMEM((reflect.shape[0], share), jnp.int32),
@@ -624,7 +662,7 @@
             pltpu.VMEM((every, lanes), F32),
             pltpu.VMEM((planes, every), F32),
             pltpu.SemaphoreType.DMA((13,)),
-            pltpu.SemaphoreType.DMA((n_chunks,)),
+            pltpu.SemaphoreType.DMA((width // LANE, n_chunks)),
             pltpu.SemaphoreType.DMA((4, n_chunks)),
             pltpu.SemaphoreType.DMA((4, n)),
             pltpu.SemaphoreType.DMA((4, n)),
@@ -647,7 +685,8 @@
     dir_cos, velocity, rate, dir_row, velocity_row, rate_row, spectrum_row, weight_row, heat,
     rising, inflow, moments, psem, sem,
 ):
-    pairs, total_rows, width = xv.shape
+    pairs, strips, total_rows, _ = xv.shape
+    width = strips * LANE
     rows = total_rows // planes
     modes = velocity.shape[1]
     dirs = pairs // modes
@@ -661,7 +700,12 @@
 
     def whole_dir(d):
         where = pl.ds(d * modes, modes)
-        return pltpu.make_async_copy(xv.at[where], out.at[where], sem.at[d, 0])
+        return [
+            pltpu.make_async_copy(
+                xv.at[where, k], out.at[where, :, pl.ds(k * LANE, LANE)], sem.at[d, k]
+            )
+            for k in range(strips)
+        ]
 
     def piece(d, b):
         return pltpu.make_async_copy(
@@ -677,7 +721,8 @@
     for copy in fetched:
         copy.start()
     for d in range(1, dirs, 2):
-        whole_dir(d).start()
+        for copy in whole_dir(d):
+            copy.start()
     for copy in fetched:
         copy.wait()
 
@@ -702,7 +747,7 @@
                             here = pl.ds(z * rows + r, SUB)
                             value = ratio * value
                             rising[d // 2 * modes + m, here, cols] = (
-                                xv[d * modes + m, here, cols] + value
+                                xv[d * modes + m, c // LANE, here, :] + value
                             )
                     return carry
 
@@ -763,7 +808,8 @@
             energy[here, cols] = (value + plain * turned) * (1.0 / pairs_total)
     for d in range(dirs):
         if d % 2:
-            whole_dir(d).wait()
+            for copy in whole_dir(d):
+                copy.wait()
         else:
             for b in range(modes // batch):
                 piece(d, b).wait()
@@ -771,13 +817,14 @@
 
 def emit_step(planes, pairs_total, scalars, heat, parts):
     xv = parts[0]
-    pairs, total_rows, width = xv.shape
+    pairs, strips, total_rows, _ = xv.shape
+    width = strips * LANE
     modes = scalars[1].shape[1]
     rows = total_rows // planes
     return pl.pallas_call(
         functools.partial(emit_kernel, planes, pairs_total),
         out_shape=(
-            jax.ShapeDtypeStruct(xv.shape, F32),
+            jax.ShapeDtypeStruct((pairs, total_rows, width), F32),
             jax.ShapeDtypeStruct((total_rows, width), F32),
         ),
         in_specs=[whole(pltpu.HBM)] * 6 + [whole()] * len(parts),
@@ -789,7 +836,7 @@
             pltpu.VMEM((min(16, modes), rows, width), F32),
             pltpu.VMEM((4, -(-(2 * planes + 2) // SUB) * SUB, LANE), F32),
             pltpu.SemaphoreType.DMA((9,)),
-            pltpu.SemaphoreType.DMA((pairs // modes, modes // min(8, modes))),
+            pltpu.SemaphoreType.DMA((pairs // modes, max(strips, modes // min(8, modes)))),
         ],
         compiler_params=pltpu.CompilerParams(vmem_limit_bytes=28 * MIB),
         name="emit_step",

time: 55.2 us -> 51.6 us (0.935)
  Pallas kernels: 53.6 us -> 50.1 us
    pallas_call x1, Pallas kernels: 46.4 us -> 42.8 us  [main_step(): pl.pallas_call(functools.partial(main_kernel, n, ns, planes), out_shape=(...]
where the time goes in v5:
time: 51.6 us; the launch traced here: 51.4 us
  Pallas kernels  50.1 us (97%)
  between operations  1.28 us (2%)
    pallas_call x1, Pallas kernels, main_step(): pl.pallas_call(functools.partial(main_kernel, n, ns, planes), out_shape=(...  42.8 us
    pallas_call x1, Pallas kernels, emit_step(): pl.pallas_call(functools.partial(emit_kernel, planes, pairs_total), out_s...  7.23 us

profile of v5, /device:TPU:0, one launch (start us, length us, event | category | flops | bytes accessed | tf_op | source)
XLA Modules:
  0.0 51.4 jit_solution(18052515584173401726)
XLA Ops:
  1.3 42.8 %main_step.1 = (f32[128,2,128,128]{3,2,1,0:T(8,128)S(1)}, f32[8,64,128]{2,1,0:T(8,128)S(1)}, f32[8,8,128]{2,1,0:T(8,128)S(1)}, f32[128,256]{1,0:T(8,128)S(1)}, f...) custom-call(s32[1]{0:T(128)S(6)} %copy.12.count, ...), custom_call_target="tpu_custom_call" | custom-call | tf_op jit(solution)/shard_map/main_step/pallas_call | solution.py:631
  44.1 7.2 %emit_step.1 = (f32[128,128,256]{2,1,0:T(8,128)}, f32[128,256]{1,0:T(8,128)}) custom-call(f32[3,32]{1,0:T(4,128)} %dir_cos_in.3, f32[1,32]{1,0:T(1,128)} %bitcast.13, f32[1,32]{1,0:T(1,128)} %bitcast.15, f32[1,32]{1,0:T(1,128)} %bitcast.17, f32[1,32]{1,0:T(1,128)} %bitcast.19, f32[16,256]{1,0:T(8,128)} %heat_in.3, ...), custom_call_target="tpu_custom_call" | custom-call | tf_op jit(solution)/shard_map/emit_step/pallas_call | solution.py:824

commit v6 on v5

--- a/solution.py
+++ b/solution.py
@@ -311,11 +311,10 @@
         low_x, low_y = splat(dir_cos[0, s]) >= 0.0, splat(dir_cos[1, s]) >= 0.0
         cx, cy, cz = cosines(d)
         shift_x = jnp.where(dir_cos[0, s] >= 0.0, 1, SUB - 1)
-        step_x = jnp.where(dir_cos[0, s] >= 0.0, -1, 1)
         shift_y = jnp.where(dir_cos[1, s] >= 0.0, 1, LANE - 1)
         head_x, tail_x = low_x & (row == 0), ~low_x & (row == SUB - 1)
         head_y, tail_y = low_y & (lane == 0), ~low_y & (lane == LANE - 1)
-        wide = 2
+        wide = 4
 
         def some(g, carry):
             sets, before = [], []
@@ -343,31 +342,22 @@
                         (r, c): xv[p, c // LANE, pl.ds(z * rows + r, SUB), :] for r, c in places
                     }
                     along = {at: pltpu.roll(own[at], shift_y, 1) for at in places}
+                    side = {at: pltpu.roll(own[at], shift_x, 0) for at in places}
                     now, ones = {}, {}
                     for r, c in places:
-                        k, at_row = c // LANE, z * rows + r
-                        under = over = None
                         if r == 0:
                             under = jnp.broadcast_to(
                                 lo[p, pl.ds(z, 1), pl.ds(c, LANE)], (SUB, LANE)
                             )
+                        else:
+                            under = side[r - SUB, c]
                         if r == last_row:
                             over = jnp.broadcast_to(
                                 hi[p, pl.ds(z, 1), pl.ds(c, LANE)], (SUB, LANE)
                             )
-                        if 0 < at_row < total_rows - SUB:
-                            one = xv[p, k, pl.ds(at_row + step_x, SUB), :]
                         else:
-                            one = pltpu.roll(own[r, c], shift_x, 0)
-                            if under is None:
-                                under = pltpu.roll(own[r - SUB, c], 1, 0)
-                            if over is None:
-                                over = pltpu.roll(own[r + SUB, c], SUB - 1, 0)
-                        if under is not None:
-                            one = jnp.where(head_x, under, one)
-                        if over is not None:
-                            one = jnp.where(tail_x, over, one)
-                        ones[r, c] = one
+                            over = side[r + SUB, c]
+                        ones[r, c] = jnp.where(head_x, under, jnp.where(tail_x, over, side[r, c]))
                     for r, c in places:
                         cols = pl.ds(c, LANE)
                         one = ones[r, c]
@@ -577,11 +567,13 @@
     closing = Reduction(acc2, slots2, part2, summed, sems2, n)
 
     tabulate()
+    find_rough()
     add_up(0)
     low = jnp.where(sp > 0, 1, 0)
     high = jnp.where(sp < ns - 1, 1, 0)
     pl.semaphore_wait(barrier, n - 1 + low + high)
     share_edges(0)
+    prepare()
     for i in range(1, len(chunks)):
         add_up(i)
         share_edges(i)
@@ -590,17 +582,12 @@
         launch(part)
         if part == 2:
             opening.combine(lambda value: squash(value * (1.0 / pairs_total)))
-    find_rough()
     slices = [(h, m) for h in range(half) for m in range(0, modes, SUB)]
-    middle = len(slices) // 2
-    for h, m in slices[:middle]:
+    for h, m in slices:
         sweep(2 * h, m, m + SUB)
-    prepare()
+    closing.start()
     opening.finish()
     choose()
-    for h, m in slices[middle:]:
-        sweep(2 * h, m, m + SUB)
-    closing.start()
     for i, (h, m) in enumerate(slices):
         settle(h, m, m + SUB)
     closing.combine(lambda value: value)

time: 51.6 us -> 48 us (0.930)
  Pallas kernels: 50.1 us -> 46.6 us
    pallas_call x1, Pallas kernels: 42.8 us -> 39.3 us  [main_step(): pl.pallas_call(functools.partial(main_kernel, n, ns, planes), out_shape=(...]
where the time goes in v6:
time: 48 us; the launch traced here: 47.8 us
  Pallas kernels  46.6 us (97%)
  between operations  1.28 us (3%)
    pallas_call x1, Pallas kernels, main_step(): pl.pallas_call(functools.partial(main_kernel, n, ns, planes), out_shape=(...  39.3 us
    pallas_call x1, Pallas kernels, emit_step(): pl.pallas_call(functools.partial(emit_kernel, planes, pairs_total), out_s...  7.23 us

profile of v6, /device:TPU:0, one launch (start us, length us, event | category | flops | bytes accessed | tf_op | source)
XLA Modules:
  0.0 47.8 jit_solution(18148649627438849820)
XLA Ops:
  1.3 39.3 %main_step.1 = (f32[128,2,128,128]{3,2,1,0:T(8,128)S(1)}, f32[8,64,128]{2,1,0:T(8,128)S(1)}, f32[8,8,128]{2,1,0:T(8,128)S(1)}, f32[128,256]{1,0:T(8,128)S(1)}, f...) custom-call(s32[1]{0:T(128)S(6)} %copy.12.count, ...), custom_call_target="tpu_custom_call" | custom-call | tf_op jit(solution)/shard_map/main_step/pallas_call | solution.py:618
  40.6 7.2 %emit_step.1 = (f32[128,128,256]{2,1,0:T(8,128)}, f32[128,256]{1,0:T(8,128)}) custom-call(f32[3,32]{1,0:T(4,128)} %dir_cos_in.3, f32[1,32]{1,0:T(1,128)} %bitcast.13, f32[1,32]{1,0:T(1,128)} %bitcast.15, f32[1,32]{1,0:T(1,128)} %bitcast.17, f32[1,32]{1,0:T(1,128)} %bitcast.19, f32[16,256]{1,0:T(8,128)} %heat_in.3, ...), custom_call_target="tpu_custom_call" | custom-call | tf_op jit(solution)/shard_map/emit_step/pallas_call | solution.py:811
